TPU v7x, 32 devices: a whole 2x2x4 slice. The times are simulated.
32 devices in a mesh: blk: 32 (over z, y, x, core).
Axes of the slice: x: 2, y: 2, z: 4, core: 2. Of those that a mesh axis runs over, the one named last changes fastest.
Arguments:
- populations: float32 [128, 27, 4096], P('blk'), may hold values from 0.6 to 1.4
- scalars: float32 [128, 9, 4096], P('blk'), may hold values from 0 to 1
- coarse_old: float32 [128, 27, 512], P('blk'), may hold values from 0.6 to 1.4
- coarse_new: float32 [128, 27, 512], P('blk'), may hold values from 0.6 to 1.4
- levels: int32 [128], replicated, may hold values 0 or 1
- neighbours: int32 [128, 6], P('blk'), may hold values from 0 to 127, as said below
- relax_rates: float32 [27], replicated, may hold values from 0.5 to 1.9
- diffusivity: float32 [9], replicated, may hold values from 0.02 to 0.15
- stoichiometry: float32 [9], replicated, may hold values from -1 to 1
Outputs:
- new_populations: float32 [128, 27, 4096], P('blk')
- new_scalars: float32 [128, 9, 4096], P('blk')
- coarse_return: float32 [128, 3456], P('blk')
Inputs may be any that keep to these rules, and one draw needn't show every extreme that they name: `neighbours`: block k lies in slot k % 4 of device k // 4. The blocks 4 * 2 * L up to 4 * 2 * (L + 1) - 1 form layer L (0 <= L < 16), held by devices 2 L and 2 L + 1; the blocks beside a block of layer L on sides 0 to 3 lie in layer L, the one on side 4 in layer L - 1 and the one on side 5 in layer L + 1, taken modulo 16. The relation is symmetric: if m is beside k on side q, k is beside m on side q xor 1. Hence the device of every listed block is at most 3 devices from the device of block k, counting cyclically over all devices.
All inputs are finite; a program needn't handle non-finite values.
Results may differ from a plain program's by a relative error of at most 0.0001.
Values sent between devices are 32-bit elements; how exact they have to be, the bound alone decides.
A program may use at most 128 MiB of HBM per device.

v0:
```python
import jax
import jax.numpy as jnp
import numpy as np
from jax import lax
from jax.sharding import PartitionSpec as P

BLOCK_EDGE = 16
HALF_EDGE = 8


PREFACTOR = 1.0
ZELDOVICH = 4.0


def shifted_2(shard, axis, by):
    devices = lax.axis_size(axis)
    return lax.ppermute(shard, axis, [(i, (i + by) % devices) for i in range(devices)])


def lattice_tables():
    steps_one = (-1.0, 0.0, 1.0)
    velocities = np.array([[a, b, c] for a in steps_one for b in steps_one for c in steps_one])
    weights = np.prod(np.where(velocities == 0, 2.0 / 3.0, 1.0 / 6.0), axis=1)
    vander = np.array([[1.0, 1.0, 1.0], [-1.0, 0.0, 1.0], [1.0, 0.0, 1.0]])
    moments = np.kron(np.kron(vander, vander), vander)
    inverse = np.array([[0.0, -0.5, 0.5], [1.0, 0.0, -1.0], [0.0, 0.5, 0.5]])
    inverse_moments = np.kron(np.kron(inverse, inverse), inverse)
    return (velocities, weights, moments, inverse_moments)


def relaxation(relax_rates):
    velocities, weights, moments, inverse_moments = lattice_tables()
    left_part = jnp.asarray(inverse_moments / weights[:, None], jnp.float32)
    right_part = jnp.asarray(moments * weights[None, :], jnp.float32)
    return jnp.dot(
        left_part * relax_rates[None, :],
        right_part,
        precision=lax.Precision.HIGHEST,
        preferred_element_type=jnp.float32,
    )


def moment_rows():
    velocities, weights, moments, inverse_moments = lattice_tables()
    return np.concatenate([weights[None, :], (velocities * weights[:, None]).T], axis=0)


def cell_stride(direction, extent):
    return extent ** (2 - direction)


def coordinate_of(direction, extent):
    return jnp.asarray(np.arange(extent**3) // cell_stride(direction, extent) % extent, jnp.int32)


def layer_of(flat, direction, upward, extent):
    index = (extent - 1) * upward
    last_axis = flat.ndim - 1
    lead = flat.shape[:-1]
    if direction == 0:
        return lax.slice_in_dim(
            flat, index * extent * extent, (index + 1) * extent * extent, axis=last_axis
        )
    if direction == 1:
        shaped = flat.reshape(lead + (extent, extent * extent))
        picked = lax.slice_in_dim(shaped, index * extent, (index + 1) * extent, axis=last_axis + 1)
        return picked.reshape(lead + (extent * extent,))
    return lax.slice_in_dim(flat, index, flat.shape[-1], stride=extent, axis=last_axis)


def spread_face(face, direction, extent):
    lead = face.shape[:-1]
    if direction == 0:
        return jnp.tile(face, (1,) * len(lead) + (extent,))
    if direction == 1:
        square_face = face.reshape(lead + (extent, extent))
        tiled = jnp.tile(square_face, (1,) * (len(lead) + 1) + (extent,))
        return tiled.reshape(lead + (extent**3,))
    return jnp.repeat(face, extent, axis=len(lead))


def move_up(flat, face, direction, extent):
    stride = cell_stride(direction, extent)
    lead = flat.shape[:-1]
    shifted = jnp.concatenate(
        [jnp.zeros(lead + (stride,), flat.dtype), flat[..., :-stride]], axis=len(lead)
    )
    return jnp.where(
        coordinate_of(direction, extent) == 0, spread_face(face, direction, extent), shifted
    )


def move_down(flat, face, direction, extent):
    stride = cell_stride(direction, extent)
    lead = flat.shape[:-1]
    shifted = jnp.concatenate(
        [flat[..., stride:], jnp.zeros(lead + (stride,), flat.dtype)], axis=len(lead)
    )
    return jnp.where(
        coordinate_of(direction, extent) == extent - 1,
        spread_face(face, direction, extent),
        shifted,
    )


def collide(lattice_state, operator_matrix):
    blocks = lattice_state.shape[0]
    velocities, weights, moments, inverse_moments = lattice_tables()
    flattened = lattice_state.reshape(blocks, 27, -1)
    moment_sums = jnp.einsum(
        "pi,bic->bpc",
        jnp.asarray(moment_rows(), jnp.float32),
        flattened,
        precision=lax.Precision.HIGHEST,
    )
    density = moment_sums[:, 0:1]
    current = moment_sums[:, 1:4]
    projected = jnp.einsum(
        "id,bdc->bic",
        jnp.asarray(velocities, jnp.float32),
        current,
        precision=lax.Precision.HIGHEST,
    )
    square = jnp.sum(current * current, axis=1, keepdims=True)
    balance = density + 3.0 * projected + 4.5 * projected * projected - 1.5 * square
    relaxed = flattened - jnp.einsum(
        "ik,bkc->bic", operator_matrix, flattened - balance, precision=lax.Precision.HIGHEST
    )
    return relaxed.reshape(lattice_state.shape)


def outgoing(relaxed, extent):
    blocks = relaxed.shape[0]
    halved = extent // 2
    face_list = []
    for facing in range(6):
        direction = facing // 2
        upward = facing % 2
        moving = lax.index_in_dim(relaxed, 2 * upward, 1 + direction, keepdims=False).reshape(
            blocks, 9, -1
        )
        layer_face = layer_of(moving, direction, upward, extent)
        grouped = layer_face.reshape(blocks, 9, halved, 2, halved, 2)
        merged = jnp.sum(grouped, axis=(3, 5)) * 0.25
        face_list.append(merged.reshape(blocks, 9, halved * halved))
    return jnp.stack(face_list, axis=1)


def enlarge(face_values, halved):
    blocks = face_values.shape[0]
    square_face = face_values.reshape(blocks, 9, halved, halved)
    grown = jnp.repeat(jnp.repeat(square_face, 2, axis=2), 2, axis=3)
    return grown.reshape(blocks, 9, 4 * halved * halved)


def crossing_faces(read, coarse_now, fine_mask, direction, extent, halved):
    blocks = read.shape[0]
    high_face = layer_of(
        lax.index_in_dim(read, 2, 1 + direction, False).reshape(blocks, 9, -1), direction, 1, extent
    )
    low_face = layer_of(
        lax.index_in_dim(read, 0, 1 + direction, False).reshape(blocks, 9, -1), direction, 0, extent
    )
    coarse_high = enlarge(
        layer_of(
            lax.index_in_dim(coarse_now, 2, 1 + direction, False).reshape(blocks, 9, -1),
            direction,
            1,
            halved,
        ),
        halved,
    )
    coarse_low = enlarge(
        layer_of(
            lax.index_in_dim(coarse_now, 0, 1 + direction, False).reshape(blocks, 9, -1),
            direction,
            0,
            halved,
        ),
        halved,
    )
    keep_fine = fine_mask[:, None, None]
    high_face = jnp.where(keep_fine, high_face, coarse_high)
    low_face = jnp.where(keep_fine, low_face, coarse_low)
    return jnp.stack([high_face, low_face], axis=1)


def apply_section(read, from_low, from_high, direction, extent):
    forward = lax.index_in_dim(read, 2, 1 + direction, False)
    backward = lax.index_in_dim(read, 0, 1 + direction, False)
    middle = lax.index_in_dim(read, 1, 1 + direction, False)
    forward = move_up(forward, from_low, direction, extent)
    backward = move_down(backward, from_high, direction, extent)
    return jnp.stack([backward, middle, forward], axis=1 + direction)


def species_rims(species, extent):
    rim_list = []
    for facing in range(6):
        rim_list.append(layer_of(species, facing // 2, facing % 2, extent))
    return jnp.stack(rim_list, axis=1)


def advance_species(species, read, halo_faces, diffusivity, stoichiometry, extent):
    blocks = species.shape[0]
    flattened = read.reshape(blocks, 27, -1)
    current = jnp.einsum(
        "pi,bic->bpc",
        jnp.asarray(moment_rows()[1:4], jnp.float32),
        flattened,
        precision=lax.Precision.HIGHEST,
    )
    drift_term = jnp.zeros_like(species)
    spread = jnp.zeros_like(species)
    for direction in range(3):
        upper_cells = move_down(species, halo_faces[:, 2 * direction + 1], direction, extent)
        lower_cells = move_up(species, halo_faces[:, 2 * direction], direction, extent)
        drift_term = drift_term + current[:, direction][:, None] * (upper_cells - lower_cells) * 0.5
        spread = spread + (upper_cells + lower_cells - 2.0 * species)
    burning = PREFACTOR * species[:, 0] * species[:, 1] * jnp.exp(ZELDOVICH * (species[:, 8] - 1.0))
    return (
        species
        - drift_term
        + diffusivity[None, :, None] * spread
        + stoichiometry[None, :, None] * burning[:, None]
    )


def send_section(payload, offset):
    return shifted_2(payload, "blk", offset)


def send_scalars(payload, offset):
    return shifted_2(payload, "blk", offset)


def send_returned(payload, offset):
    return shifted_2(payload, "blk", offset)


def collect(payload, sender, offsets_list):
    pieces = []
    for offset in offsets_list:
        pieces.append(payload if offset == 0 else sender(payload, offset))
    return jnp.stack(pieces, axis=0)


def side_values(table, sender, distance, positions, near_offsets):
    base = -near_offsets[0]
    nearby = collect(table[:, 0:4], sender, near_offsets)
    below = collect(table[:, 5], sender, (1, 2, 3))
    above = collect(table[:, 4], sender, (-1, -2, -3))
    values = [
        nearby[distance[:, facing] + base, positions[:, facing], facing ^ 1] for facing in range(4)
    ]
    values.append(below[distance[:, 4] - 1, positions[:, 4]])
    values.append(above[-distance[:, 5] - 1, positions[:, 5]])
    return values


def local(
    populations,
    scalars,
    coarse_old,
    coarse_new,
    levels,
    neighbours,
    relax_rates,
    diffusivity,
    stoichiometry,
):
    slot_count = populations.shape[0]
    extent = BLOCK_EDGE
    halved = HALF_EDGE
    devices = lax.axis_size("blk")
    device_index = lax.axis_index("blk")
    near_offsets = (-1, 0, 1)
    base = -near_offsets[0]
    own_levels = lax.dynamic_slice_in_dim(levels, device_index * slot_count, slot_count)
    fine_mask = own_levels == 1
    neighbour_fine = levels[neighbours] == 1
    owners = neighbours // slot_count
    positions = neighbours % slot_count
    distance = (device_index - owners) % devices
    distance = jnp.where(distance > devices // 2, distance - devices, distance)
    operator_matrix = relaxation(relax_rates)
    lattice_state = populations.reshape(slot_count, 3, 3, 3, -1)
    species = scalars
    old_coarse = coarse_old.reshape(slot_count, 3, 3, 3, -1)
    new_coarse = coarse_new.reshape(slot_count, 3, 3, 3, -1)
    returned = jnp.zeros((slot_count, 6, 9, halved * halved), jnp.float32)
    for substep in range(2):
        coarse_now = old_coarse if substep == 0 else 0.5 * (old_coarse + new_coarse)
        relaxed = collide(lattice_state, operator_matrix)
        returned = returned + 0.5 * jnp.where(
            fine_mask[:, None, None, None], outgoing(relaxed, extent), 0.0
        )
        read = relaxed
        for direction in range(3):
            low_column = 2 * direction
            high_column = low_column + 1
            table = crossing_faces(read, coarse_now, fine_mask, direction, extent, halved)
            if direction == 2:
                low_stack = collect(table[:, 0], send_section, (1, 2, 3))
                high_stack = collect(table[:, 1], send_section, (-1, -2, -3))
                from_low = low_stack[distance[:, low_column] - 1, positions[:, low_column]]
                from_high = high_stack[-distance[:, high_column] - 1, positions[:, high_column]]
            else:
                stacked = collect(table, send_section, near_offsets)
                from_low = stacked[distance[:, low_column] + base, positions[:, low_column], 0]
                from_high = stacked[distance[:, high_column] + base, positions[:, high_column], 1]
            from_low = from_low.reshape(slot_count, 3, 3, extent * extent)
            from_high = from_high.reshape(slot_count, 3, 3, extent * extent)
            read = apply_section(read, from_low, from_high, direction, extent)
        rim_faces = species_rims(species, extent)
        received_list = side_values(rim_faces, send_scalars, distance, positions, near_offsets)
        halo_list = []
        for facing in range(6):
            halo_list.append(
                jnp.where(
                    neighbour_fine[:, facing][:, None, None],
                    received_list[facing],
                    rim_faces[:, facing],
                )
            )
        species = advance_species(
            species, read, jnp.stack(halo_list, axis=1), diffusivity, stoichiometry, extent
        )
        lattice_state = read
    coarse_list = side_values(returned, send_returned, distance, positions, near_offsets)
    coarse_return = jnp.where(
        fine_mask[:, None, None, None], 0.0, jnp.stack(coarse_list, axis=1)
    ).reshape(slot_count, -1)
    new_populations = jnp.where(
        fine_mask[:, None, None], lattice_state.reshape(populations.shape), populations
    )
    new_scalars = jnp.where(fine_mask[:, None, None], species, scalars)
    return (new_populations, new_scalars, coarse_return)


def solution(mesh):
    in_specs = (
        P("blk", None, None),
        P("blk", None, None),
        P("blk", None, None),
        P("blk", None, None),
        P(),
        P("blk", None),
        P(),
        P(),
        P(),
    )
    out_specs = (P("blk", None, None), P("blk", None, None), P("blk", None))
    return jax.shard_map(local, mesh=mesh, in_specs=in_specs, out_specs=out_specs, check_vma=False)
```

profile of v0, /device:TPU:0, one launch (start us, length us, event | category | flops | bytes accessed | tf_op | source)
XLA Modules:
  0.0 558.3 jit_solution(1464038444247205480)
XLA Ops:
  0.7 3.2 slice.601
  3.8 5.5 collective-permute-start.24
  10.8 3.0 slice.602
  35.9 4.4 fusion.1
  58.0 3.0 slice.632
  109.5 5.2 collective-permute-start.22
  114.7 5.3 collective-permute-start.20
  123.0 5.3 collective-permute-start
  143.9 5.5 collective-permute-start.2
  150.3 3.3 broadcast_in_dim.460
  153.6 4.8 reshape.518
  158.4 3.3 broadcast_in_dim.464
  161.7 4.8 reshape.519
  173.4 4.1 tile.144
  177.6 3.5 tile.146
  181.1 4.8 tile.147
  189.3 3.0 slice.536
  221.5 4.8 tile.165
  228.9 4.8 tile.167
  235.6 5.5 collective-permute-done.7
  242.7 3.3 broadcast_in_dim.425
  246.0 4.1 reshape.496
  250.1 3.3 broadcast_in_dim.421
  253.4 4.5 reshape.492
  265.2 4.4 fusion
  275.4 5.5 collective-permute-start.10
  284.5 3.0 slice.642
  287.5 3.0 slice.640
  349.9 3.2 convolution_bitcast_fusion.5
  353.6 3.6 multiply_add_fusion
  388.1 5.4 collective-permute-start.32
  397.5 3.8 collective-permute-start.28
  402.0 3.3 broadcast_in_dim.470
  405.3 4.8 reshape.521
  410.0 3.3 broadcast_in_dim.472
  413.3 4.8 reshape.522
  442.8 5.5 collective-permute-start.12
  468.4 4.8 tile.156
  475.7 4.8 tile.159
  494.6 3.5 tile.172
  498.1 4.8 tile.173
  502.9 3.5 tile.174
  506.4 4.8 tile.175
  529.9 3.3 broadcast_in_dim.442
  533.2 4.8 reshape.515
  538.0 4.0 broadcast_in_dim.438
  542.0 4.8 reshape.511
  555.4 2.7 add_select_fusion
  (682 shorter events, 353.1 us)
Async XLA Ops:
  0.6 25.8 %copy-start.93 = (f32[4,27,1]{1,0,2:T(4,128)S(1)}, f32[4,27,1]{1,0,2:T(4,128)}, u32[]{:S(2)}) copy-start(f32[4,27,1]{1,0,2:T(4,128)} %constant.734) | copy-start | bytes 1300
  0.6 25.8 %copy-start.2 = (f32[4,27,4096]{2,0,1:T(4,128)S(1)}, f32[4,27,4096]{2,0,1:T(4,128)}, u32[]{:S(2)}) copy-start(f32[4,27,4096]{2,0,1:T(4,128)} %param.41) | copy-start | bytes 5308420
  3.8 119.2 %collective-permute-start.24 = (f32[4,9,256]{2,0,1:T(4,128)}, f32[4,9,256]{2,0,1:T(4,128)}, u32[]{:S(2)}, u32[]{:S(2)}) collective-permute-start(f32[4,9,256]{2,0,1:T(4,128)} %slice.601), channel_id=1, source_target_pairs={{0,29},{1,30},{2,31},{3,0},{4,1},{5,2},{6,3},{7,4},{8,5},{9,6},{10... | collective-permute-start | bytes 110600 | tf_op jit(solution)/shard_map/ppermute | solution.py:17
  9.3 113.7 %collective-permute-start.23 = (f32[4,9,256]{2,0,1:T(4,128)}, f32[4,9,256]{2,0,1:T(4,128)}, u32[]{:S(2)}, u32[]{:S(2)}) collective-permute-start(f32[4,9,256]{2,0,1:T(4,128)} %slice.601), channel_id=1, source_target_pairs={{0,30},{1,31},{2,0},{3,1},{4,2},{5,3},{6,4},{7,5},{8,6},{9,7},{10,... | collective-permute-start | bytes 110600 | tf_op jit(solution)/shard_map/ppermute | solution.py:17
  13.8 95.7 %collective-permute-start.27 = (f32[4,9,256]{2,0,1:T(4,128)}, f32[4,9,256]{2,0,1:T(4,128)}, u32[]{:S(2)}, u32[]{:S(2)}) collective-permute-start(f32[4,9,256]{2,0,1:T(4,128)} %slice.602), channel_id=1, source_target_pairs={{0,3},{1,4},{2,5},{3,6},{4,7},{5,8},{6,9},{7,10},{8,11},{9,12},{10... | collective-permute-start | bytes 110600 | tf_op jit(solution)/shard_map/ppermute | solution.py:17
  15.3 99.4 %collective-permute-start.26 = (f32[4,9,256]{2,0,1:T(4,128)}, f32[4,9,256]{2,0,1:T(4,128)}, u32[]{:S(2)}, u32[]{:S(2)}) collective-permute-start(f32[4,9,256]{2,0,1:T(4,128)} %slice.602), channel_id=1, source_target_pairs={{0,2},{1,3},{2,4},{3,5},{4,6},{5,7},{6,8},{7,9},{8,10},{9,11},{10,... | collective-permute-start | bytes 110600 | tf_op jit(solution)/shard_map/ppermute | solution.py:17
  15.3 99.4 %collective-permute-start.25 = (f32[4,9,256]{2,0,1:T(4,128)}, f32[4,9,256]{2,0,1:T(4,128)}, u32[]{:S(2)}, u32[]{:S(2)}) collective-permute-start(f32[4,9,256]{2,0,1:T(4,128)} %slice.602), channel_id=1, source_target_pairs={{0,1},{1,2},{2,3},{3,4},{4,5},{5,6},{6,7},{7,8},{8,9},{9,10},{10,1... | collective-permute-start | bytes 110600 | tf_op jit(solution)/shard_map/ppermute | solution.py:17
  84.7 46.9 %copy-start.85 = (s32[4]{0:T(128)}, s32[4]{0:T(128)S(1)}, u32[]{:S(2)}) copy-start(s32[4]{0:T(128)S(1)} %get-tuple-element.147) | copy-start | bytes 52
  109.5 18.8 %collective-permute-start.22 = (f32[4,9,256]{2,0,1:T(4,128)}, f32[4,9,256]{2,0,1:T(4,128)S(1)}, u32[]{:S(2)}, u32[]{:S(2)}) collective-permute-start(f32[4,9,256]{2,0,1:T(4,128)} %slice.601), channel_id=1, source_target_pairs={{0,31},{1,0},{2,1},{3,2},{4,3},{5,4},{6,5},{7,6},{8,7},{9,8},{10,9... | collective-permute-start | bytes 110600 | tf_op jit(solution)/shard_map/ppermute | solution.py:17
  114.7 82.1 %collective-permute-start.21 = (f32[4,4,9,256]{3,0,2,1:T(4,128)}, f32[4,4,9,256]{3,0,2,1:T(4,128)}, u32[]{:S(2)}, u32[]{:S(2)}) collective-permute-start(f32[4,4,9,256]{3,0,2,1:T(4,128)} %get-tuple-element.119), channel_id=1, source_target_pairs={{0,1},{1,2},{2,3},{3,4},{4,5},{5,6},{6,7},{7,8},{8,9},{9,10},{10,1... | collective-permute-start | bytes 442376 | tf_op jit(solution)/shard_map/ppermute | solution.py:17
  114.7 83.6 %collective-permute-start.20 = (f32[4,4,9,256]{3,0,2,1:T(4,128)}, f32[4,4,9,256]{3,0,2,1:T(4,128)}, u32[]{:S(2)}, u32[]{:S(2)}) collective-permute-start(f32[4,4,9,256]{3,0,2,1:T(4,128)} %get-tuple-element.119), channel_id=1, source_target_pairs={{0,31},{1,0},{2,1},{3,2},{4,3},{5,4},{6,5},{7,6},{8,7},{9,8},{10,9... | collective-permute-start | bytes 442376 | tf_op jit(solution)/shard_map/ppermute | solution.py:17
  123.0 8.0 %collective-permute-start.1 = (f32[4,2,9,256]{3,2,1,0:T(8,128)S(1)}, f32[4,2,9,256]{3,2,1,0:T(8,128)S(1)}, u32[]{:S(2)}, u32[]{:S(2)}) collective-permute-start(f32[4,2,9,256]{3,2,1,0:T(8,128)S(1)} %copy-done.60), channel_id=1, source_target_pairs={{0,1},{1,2},{2,3},{3,4},{4,5},{5,6},{6,7},{7,8},{8,9},{9,10},{10,1... | collective-permute-start | bytes 221192 | tf_op jit(solution)/shard_map/ppermute | solution.py:17
  123.0 8.0 %collective-permute-start = (f32[4,2,9,256]{3,2,1,0:T(8,128)S(1)}, f32[4,2,9,256]{3,2,1,0:T(8,128)S(1)}, u32[]{:S(2)}, u32[]{:S(2)}) collective-permute-start(f32[4,2,9,256]{3,2,1,0:T(8,128)S(1)} %copy-done.60), channel_id=1, source_target_pairs={{0,31},{1,0},{2,1},{3,2},{4,3},{5,4},{6,5},{7,6},{8,7},{9,8},{10,9... | collective-permute-start | bytes 221192 | tf_op jit(solution)/shard_map/ppermute | solution.py:17
  143.9 23.0 %collective-permute-start.3 = (f32[4,2,9,256]{3,2,1,0:T(8,128)}, f32[4,2,9,256]{3,2,1,0:T(8,128)}, u32[]{:S(2)}, u32[]{:S(2)}) collective-permute-start(f32[4,2,9,256]{3,2,1,0:T(8,128)} %get-tuple-element.125), channel_id=1, source_target_pairs={{0,1},{1,2},{2,3},{3,4},{4,5},{5,6},{6,7},{7,8},{8,9},{9,10},{10,1... | collective-permute-start | bytes 221192 | tf_op jit(solution)/shard_map/ppermute | solution.py:17
  143.9 23.0 %collective-permute-start.2 = (f32[4,2,9,256]{3,2,1,0:T(8,128)}, f32[4,2,9,256]{3,2,1,0:T(8,128)}, u32[]{:S(2)}, u32[]{:S(2)}) collective-permute-start(f32[4,2,9,256]{3,2,1,0:T(8,128)} %get-tuple-element.125), channel_id=1, source_target_pairs={{0,31},{1,0},{2,1},{3,2},{4,3},{5,4},{6,5},{7,6},{8,7},{9,8},{10,9... | collective-permute-start | bytes 221192 | tf_op jit(solution)/shard_map/ppermute | solution.py:17
  196.0 37.6 %collective-permute-start.6 = (f32[4,9,256]{2,1,0:T(8,128)}, f32[4,9,256]{2,1,0:T(8,128)}, u32[]{:S(2)}, u32[]{:S(2)}) collective-permute-start(f32[4,9,256]{2,1,0:T(8,128)} %get-tuple-element.141), channel_id=1, source_target_pairs={{0,29},{1,30},{2,31},{3,0},{4,1},{5,2},{6,3},{7,4},{8,5},{9,6},{10... | collective-permute-start | bytes 110600 | tf_op jit(solution)/shard_map/ppermute | solution.py:17
  196.0 38.0 %collective-permute-start.5 = (f32[4,9,256]{2,1,0:T(8,128)}, f32[4,9,256]{2,1,0:T(8,128)}, u32[]{:S(2)}, u32[]{:S(2)}) collective-permute-start(f32[4,9,256]{2,1,0:T(8,128)} %get-tuple-element.141), channel_id=1, source_target_pairs={{0,30},{1,31},{2,0},{3,1},{4,2},{5,3},{6,4},{7,5},{8,6},{9,7},{10,... | collective-permute-start | bytes 110600 | tf_op jit(solution)/shard_map/ppermute | solution.py:17
  196.7 37.4 %collective-permute-start.4 = (f32[4,9,256]{2,1,0:T(8,128)}, f32[4,9,256]{2,1,0:T(8,128)}, u32[]{:S(2)}, u32[]{:S(2)}) collective-permute-start(f32[4,9,256]{2,1,0:T(8,128)} %get-tuple-element.141), channel_id=1, source_target_pairs={{0,31},{1,0},{2,1},{3,2},{4,3},{5,4},{6,5},{7,6},{8,7},{9,8},{10,9... | collective-permute-start | bytes 110600 | tf_op jit(solution)/shard_map/ppermute | solution.py:17
  196.8 38.7 %collective-permute-start.9 = (f32[4,9,256]{2,1,0:T(8,128)}, f32[4,9,256]{2,1,0:T(8,128)}, u32[]{:S(2)}, u32[]{:S(2)}) collective-permute-start(f32[4,9,256]{2,1,0:T(8,128)} %get-tuple-element.142), channel_id=1, source_target_pairs={{0,3},{1,4},{2,5},{3,6},{4,7},{5,8},{6,9},{7,10},{8,11},{9,12},{10... | collective-permute-start | bytes 110600 | tf_op jit(solution)/shard_map/ppermute | solution.py:17
  198.4 37.2 %collective-permute-start.8 = (f32[4,9,256]{2,1,0:T(8,128)}, f32[4,9,256]{2,1,0:T(8,128)}, u32[]{:S(2)}, u32[]{:S(2)}) collective-permute-start(f32[4,9,256]{2,1,0:T(8,128)} %get-tuple-element.142), channel_id=1, source_target_pairs={{0,2},{1,3},{2,4},{3,5},{4,6},{5,7},{6,8},{7,9},{8,10},{9,11},{10,... | collective-permute-start | bytes 110600 | tf_op jit(solution)/shard_map/ppermute | solution.py:17
  233.7 7.5 %collective-permute-start.7 = (f32[4,9,256]{2,1,0:T(8,128)}, f32[4,9,256]{2,1,0:T(8,128)S(1)}, u32[]{:S(2)}, u32[]{:S(2)}) collective-permute-start(f32[4,9,256]{2,1,0:T(8,128)} %get-tuple-element.142), channel_id=1, source_target_pairs={{0,1},{1,2},{2,3},{3,4},{4,5},{5,6},{6,7},{7,8},{8,9},{9,10},{10,1... | collective-permute-start | bytes 110600 | tf_op jit(solution)/shard_map/ppermute | solution.py:17
  275.4 142.7 %collective-permute-start.11 = (f32[4,2,9,256]{3,2,0,1:T(8,128)}, f32[4,2,9,256]{3,2,0,1:T(8,128)}, u32[]{:S(2)}, u32[]{:S(2)}) collective-permute-start(f32[4,2,9,256]{3,2,0,1:T(8,128)} %get-tuple-element.123), channel_id=1, source_target_pairs={{0,1},{1,2},{2,3},{3,4},{4,5},{5,6},{6,7},{7,8},{8,9},{9,10},{10,1... | collective-permute-start | bytes 221192 | tf_op jit(solution)/shard_map/ppermute | solution.py:17
  275.4 142.7 %collective-permute-start.10 = (f32[4,2,9,256]{3,2,0,1:T(8,128)}, f32[4,2,9,256]{3,2,0,1:T(8,128)}, u32[]{:S(2)}, u32[]{:S(2)}) collective-permute-start(f32[4,2,9,256]{3,2,0,1:T(8,128)} %get-tuple-element.123), channel_id=1, source_target_pairs={{0,31},{1,0},{2,1},{3,2},{4,3},{5,4},{6,5},{7,6},{8,7},{9,8},{10,9... | collective-permute-start | bytes 221192 | tf_op jit(solution)/shard_map/ppermute | solution.py:17
  348.8 21.5 %collective-permute-start.43 = (f32[4,9,64]{2,1,0:T(8,128)}, f32[4,9,64]{2,1,0:T(8,128)}, u32[]{:S(2)}, u32[]{:S(2)}) collective-permute-start(f32[4,9,64]{2,1,0:T(8,128)} %get-tuple-element.112), channel_id=1, source_target_pairs={{0,29},{1,30},{2,31},{3,0},{4,1},{5,2},{6,3},{7,4},{8,5},{9,6},{10... | collective-permute-start | bytes 27656 | tf_op jit(solution)/shard_map/ppermute | solution.py:17
  348.8 23.5 %collective-permute-start.42 = (f32[4,9,64]{2,1,0:T(8,128)}, f32[4,9,64]{2,1,0:T(8,128)}, u32[]{:S(2)}, u32[]{:S(2)}) collective-permute-start(f32[4,9,64]{2,1,0:T(8,128)} %get-tuple-element.112), channel_id=1, source_target_pairs={{0,30},{1,31},{2,0},{3,1},{4,2},{5,3},{6,4},{7,5},{8,6},{9,7},{10,... | collective-permute-start | bytes 27656 | tf_op jit(solution)/shard_map/ppermute | solution.py:17
  348.9 25.6 %collective-permute-start.41 = (f32[4,9,64]{2,1,0:T(8,128)}, f32[4,9,64]{2,1,0:T(8,128)}, u32[]{:S(2)}, u32[]{:S(2)}) collective-permute-start(f32[4,9,64]{2,1,0:T(8,128)} %get-tuple-element.112), channel_id=1, source_target_pairs={{0,31},{1,0},{2,1},{3,2},{4,3},{5,4},{6,5},{7,6},{8,7},{9,8},{10,9... | collective-permute-start | bytes 27656 | tf_op jit(solution)/shard_map/ppermute | solution.py:17
  370.2 25.2 %copy-start.99 = (pred[4]{0:T(512)(128)(4,1)S(1)}, pred[4]{0:T(512)(128)(4,1)}, u32[]{:S(2)}) copy-start(pred[4]{0:T(512)(128)(4,1)} %get-tuple-element.29) | copy-start | bytes 16
  370.2 6.1 %collective-permute-start.40 = (f32[4,9,64]{2,1,0:T(8,128)S(1)}, f32[4,9,64]{2,1,0:T(8,128)S(1)}, u32[]{:S(2)}, u32[]{:S(2)}) collective-permute-start(f32[4,9,64]{2,1,0:T(8,128)S(1)} %copy-done.89), channel_id=1, source_target_pairs={{0,3},{1,4},{2,5},{3,6},{4,7},{5,8},{6,9},{7,10},{8,11},{9,12},{10... | collective-permute-start | bytes 27656 | tf_op jit(solution)/shard_map/ppermute | solution.py:17
  372.3 7.7 %collective-permute-start.39 = (f32[4,9,64]{2,1,0:T(8,128)S(1)}, f32[4,9,64]{2,1,0:T(8,128)S(1)}, u32[]{:S(2)}, u32[]{:S(2)}) collective-permute-start(f32[4,9,64]{2,1,0:T(8,128)S(1)} %copy-done.89), channel_id=1, source_target_pairs={{0,2},{1,3},{2,4},{3,5},{4,6},{5,7},{6,8},{7,9},{8,10},{9,11},{10,... | collective-permute-start | bytes 27656 | tf_op jit(solution)/shard_map/ppermute | solution.py:17
  374.5 7.1 %collective-permute-start.38 = (f32[4,9,64]{2,1,0:T(8,128)S(1)}, f32[4,9,64]{2,1,0:T(8,128)S(1)}, u32[]{:S(2)}, u32[]{:S(2)}) collective-permute-start(f32[4,9,64]{2,1,0:T(8,128)S(1)} %copy-done.89), channel_id=1, source_target_pairs={{0,1},{1,2},{2,3},{3,4},{4,5},{5,6},{6,7},{7,8},{8,9},{9,10},{10,1... | collective-permute-start | bytes 27656 | tf_op jit(solution)/shard_map/ppermute | solution.py:17
  376.3 8.0 %collective-permute-start.37 = (f32[4,4,9,64]{3,2,1,0:T(8,128)S(1)}, f32[4,4,9,64]{3,2,1,0:T(8,128)S(1)}, u32[]{:S(2)}, u32[]{:S(2)}) collective-permute-start(f32[4,4,9,64]{3,2,1,0:T(8,128)S(1)} %copy-done.61), channel_id=1, source_target_pairs={{0,1},{1,2},{2,3},{3,4},{4,5},{5,6},{6,7},{7,8},{8,9},{9,10},{10,1... | collective-permute-start | bytes 110600 | tf_op jit(solution)/shard_map/ppermute | solution.py:17
  380.0 4.3 collective-permute-start.36
  381.7 6.4 %collective-permute-start.35 = (f32[4,9,256]{2,0,1:T(4,128)S(1)}, f32[4,9,256]{2,0,1:T(4,128)S(1)}, u32[]{:S(2)}, u32[]{:S(2)}) collective-permute-start(f32[4,9,256]{2,0,1:T(4,128)S(1)} %slice.621), channel_id=1, source_target_pairs={{0,3},{1,4},{2,5},{3,6},{4,7},{5,8},{6,9},{7,10},{8,11},{9,12},{10... | collective-permute-start | bytes 110600 | tf_op jit(solution)/shard_map/ppermute | solution.py:17
  384.3 9.2 %collective-permute-start.34 = (f32[4,9,256]{2,0,1:T(4,128)S(1)}, f32[4,9,256]{2,0,1:T(4,128)S(1)}, u32[]{:S(2)}, u32[]{:S(2)}) collective-permute-start(f32[4,9,256]{2,0,1:T(4,128)S(1)} %slice.621), channel_id=1, source_target_pairs={{0,2},{1,3},{2,4},{3,5},{4,6},{5,7},{6,8},{7,9},{8,10},{9,11},{10,... | collective-permute-start | bytes 110600 | tf_op jit(solution)/shard_map/ppermute | solution.py:17
  384.3 9.2 %collective-permute-start.33 = (f32[4,9,256]{2,0,1:T(4,128)S(1)}, f32[4,9,256]{2,0,1:T(4,128)S(1)}, u32[]{:S(2)}, u32[]{:S(2)}) collective-permute-start(f32[4,9,256]{2,0,1:T(4,128)S(1)} %slice.621), channel_id=1, source_target_pairs={{0,1},{1,2},{2,3},{3,4},{4,5},{5,6},{6,7},{7,8},{8,9},{9,10},{10,1... | collective-permute-start | bytes 110600 | tf_op jit(solution)/shard_map/ppermute | solution.py:17
  388.1 7.4 %collective-permute-start.32 = (f32[4,9,256]{2,0,1:T(4,128)S(1)}, f32[4,9,256]{2,0,1:T(4,128)S(1)}, u32[]{:S(2)}, u32[]{:S(2)}) collective-permute-start(f32[4,9,256]{2,0,1:T(4,128)S(1)} %slice.620), channel_id=1, source_target_pairs={{0,29},{1,30},{2,31},{3,0},{4,1},{5,2},{6,3},{7,4},{8,5},{9,6},{10... | collective-permute-start | bytes 110600 | tf_op jit(solution)/shard_map/ppermute | solution.py:17
  393.5 4.0 collective-permute-start.31
  393.5 7.7 %collective-permute-start.30 = (f32[4,9,256]{2,0,1:T(4,128)S(1)}, f32[4,9,256]{2,0,1:T(4,128)S(1)}, u32[]{:S(2)}, u32[]{:S(2)}) collective-permute-start(f32[4,9,256]{2,0,1:T(4,128)S(1)} %slice.620), channel_id=1, source_target_pairs={{0,31},{1,0},{2,1},{3,2},{4,3},{5,4},{6,5},{7,6},{8,7},{9,8},{10,9... | collective-permute-start | bytes 110600 | tf_op jit(solution)/shard_map/ppermute | solution.py:17
  395.5 54.0 %collective-permute-start.29 = (f32[4,4,9,256]{3,0,2,1:T(4,128)}, f32[4,4,9,256]{3,0,2,1:T(4,128)}, u32[]{:S(2)}, u32[]{:S(2)}) collective-permute-start(f32[4,4,9,256]{3,0,2,1:T(4,128)} %get-tuple-element.117), channel_id=1, source_target_pairs={{0,1},{1,2},{2,3},{3,4},{4,5},{5,6},{6,7},{7,8},{8,9},{9,10},{10,1... | collective-permute-start | bytes 442376 | tf_op jit(solution)/shard_map/ppermute | solution.py:17
  397.5 52.0 %collective-permute-start.28 = (f32[4,4,9,256]{3,0,2,1:T(4,128)}, f32[4,4,9,256]{3,0,2,1:T(4,128)}, u32[]{:S(2)}, u32[]{:S(2)}) collective-permute-start(f32[4,4,9,256]{3,0,2,1:T(4,128)} %get-tuple-element.117), channel_id=1, source_target_pairs={{0,31},{1,0},{2,1},{3,2},{4,3},{5,4},{6,5},{7,6},{8,7},{9,8},{10,9... | collective-permute-start | bytes 442376 | tf_op jit(solution)/shard_map/ppermute | solution.py:17
  442.8 20.3 %collective-permute-start.13 = (f32[4,2,9,256]{3,2,1,0:T(8,128)}, f32[4,2,9,256]{3,2,1,0:T(8,128)}, u32[]{:S(2)}, u32[]{:S(2)}) collective-permute-start(f32[4,2,9,256]{3,2,1,0:T(8,128)} %get-tuple-element.121), channel_id=1, source_target_pairs={{0,1},{1,2},{2,3},{3,4},{4,5},{5,6},{6,7},{7,8},{8,9},{9,10},{10,1... | collective-permute-start | bytes 221192 | tf_op jit(solution)/shard_map/ppermute | solution.py:17
  442.8 20.3 %collective-permute-start.12 = (f32[4,2,9,256]{3,2,1,0:T(8,128)}, f32[4,2,9,256]{3,2,1,0:T(8,128)}, u32[]{:S(2)}, u32[]{:S(2)}) collective-permute-start(f32[4,2,9,256]{3,2,1,0:T(8,128)} %get-tuple-element.121), channel_id=1, source_target_pairs={{0,31},{1,0},{2,1},{3,2},{4,3},{5,4},{6,5},{7,6},{8,7},{9,8},{10,9... | collective-permute-start | bytes 221192 | tf_op jit(solution)/shard_map/ppermute | solution.py:17
  489.4 28.3 %collective-permute-start.16 = (f32[4,9,256]{2,1,0:T(8,128)}, f32[4,9,256]{2,1,0:T(8,128)}, u32[]{:S(2)}, u32[]{:S(2)}) collective-permute-start(f32[4,9,256]{2,1,0:T(8,128)} %get-tuple-element.135), channel_id=1, source_target_pairs={{0,29},{1,30},{2,31},{3,0},{4,1},{5,2},{6,3},{7,4},{8,5},{9,6},{10... | collective-permute-start | bytes 110600 | tf_op jit(solution)/shard_map/ppermute | solution.py:17
  489.4 28.7 %collective-permute-start.15 = (f32[4,9,256]{2,1,0:T(8,128)}, f32[4,9,256]{2,1,0:T(8,128)}, u32[]{:S(2)}, u32[]{:S(2)}) collective-permute-start(f32[4,9,256]{2,1,0:T(8,128)} %get-tuple-element.135), channel_id=1, source_target_pairs={{0,30},{1,31},{2,0},{3,1},{4,2},{5,3},{6,4},{7,5},{8,6},{9,7},{10,... | collective-permute-start | bytes 110600 | tf_op jit(solution)/shard_map/ppermute | solution.py:17
  489.4 28.7 %collective-permute-start.14 = (f32[4,9,256]{2,1,0:T(8,128)}, f32[4,9,256]{2,1,0:T(8,128)}, u32[]{:S(2)}, u32[]{:S(2)}) collective-permute-start(f32[4,9,256]{2,1,0:T(8,128)} %get-tuple-element.135), channel_id=1, source_target_pairs={{0,31},{1,0},{2,1},{3,2},{4,3},{5,4},{6,5},{7,6},{8,7},{9,8},{10,9... | collective-permute-start | bytes 110600 | tf_op jit(solution)/shard_map/ppermute | solution.py:17
  511.2 12.1 %collective-permute-start.19 = (f32[4,9,256]{2,1,0:T(8,128)}, f32[4,9,256]{2,1,0:T(8,128)}, u32[]{:S(2)}, u32[]{:S(2)}) collective-permute-start(f32[4,9,256]{2,1,0:T(8,128)} %get-tuple-element.136), channel_id=1, source_target_pairs={{0,3},{1,4},{2,5},{3,6},{4,7},{5,8},{6,9},{7,10},{8,11},{9,12},{10... | collective-permute-start | bytes 110600 | tf_op jit(solution)/shard_map/ppermute | solution.py:17
  513.2 10.1 %collective-permute-start.18 = (f32[4,9,256]{2,1,0:T(8,128)}, f32[4,9,256]{2,1,0:T(8,128)}, u32[]{:S(2)}, u32[]{:S(2)}) collective-permute-start(f32[4,9,256]{2,1,0:T(8,128)} %get-tuple-element.136), channel_id=1, source_target_pairs={{0,2},{1,3},{2,4},{3,5},{4,6},{5,7},{6,8},{7,9},{8,10},{9,11},{10,... | collective-permute-start | bytes 110600 | tf_op jit(solution)/shard_map/ppermute | solution.py:17
  517.7 7.6 %collective-permute-start.17 = (f32[4,9,256]{2,1,0:T(8,128)}, f32[4,9,256]{2,1,0:T(8,128)}, u32[]{:S(2)}, u32[]{:S(2)}) collective-permute-start(f32[4,9,256]{2,1,0:T(8,128)} %get-tuple-element.136), channel_id=1, source_target_pairs={{0,1},{1,2},{2,3},{3,4},{4,5},{5,6},{6,7},{7,8},{8,9},{9,10},{10,1... | collective-permute-start | bytes 110600 | tf_op jit(solution)/shard_map/ppermute | solution.py:17
  (103 other events, 518.1 us)
where the time goes:
time: 567 us; the launch traced here: 558 us
  local copies, waits for them, and re-layouts  357 us (63%)
  other arithmetic  90.2 us (16%)
  starting transfers between devices  70.2 us (12%)
  matrix products  22.8 us (4%)
  waiting for transfers between devices  14.5 us (3%)
    ppermute x44, starting transfers between devices, shifted_2(): lax.ppermute(shard, axis, [(i, (i + by) % devices) for i in range(devices)])  70.2 us
    another operation x20, local copies, waits for them, and re-layouts, spread_face(): tiled = jnp.tile(square_face, (1,) * (len(lead) + 1) + (extent,))  62.4 us
    slice x20, local copies, waits for them, and re-layouts, layer_of(): lax.slice_in_dim(flat, index, flat.shape[-1], stride=extent, axis=last_axis)  39.2 us
    reshape x8, local copies, waits for them, and re-layouts, spread_face(): return jnp.repeat(face, extent, axis=len(lead))  37.4 us
    broadcast_in_dim x8, local copies, waits for them, and re-layouts, spread_face(): return jnp.repeat(face, extent, axis=len(lead))  27 us
    gather x20, local copies, waits for them, and re-layouts, side_values(): nearby[distance[:, facing] + base, positions[:, facing], facing ^ 1]  22.2 us
    another operation x23, other arithmetic, collect(): return jnp.stack(pieces, axis=0)  18.2 us
    slice x20, local copies, waits for them, and re-layouts, layer_of(): lax.slice_in_dim(shaped, index * extent, (index + 1) * extent, axis=last_...  18 us
  transfers between devices with their start and end apart: 44, of which 8 were waited for; matrix products, arithmetic and copies ran while one was open for 67% of the time, Pallas kernels for 0%

commit v1 on v0

v1 whole, which is shorter than its diff:
```python
import jax
import jax.numpy as jnp
import numpy as np
from jax import lax
from jax.experimental import pallas as pl
from jax.experimental.pallas import tpu as pltpu
from jax.sharding import PartitionSpec as P

F32 = jnp.float32
MESH = pl.DeviceIdType.MESH
LANES = 128
ROWS = 32
HALF = 16
MOVERS = (
    (tuple(18 + p for p in range(9)), tuple(p for p in range(9))),
    (
        tuple(9 * (p // 3) + 6 + p % 3 for p in range(9)),
        tuple(9 * (p // 3) + p % 3 for p in range(9)),
    ),
    (tuple(3 * p + 2 for p in range(9)), tuple(3 * p for p in range(9))),
)
SCALAR_ROWS = (tuple(range(9)), tuple(range(9)))
XR = 40
POP_ROWS = 36 * 32
SCA_ROWS = 20 * 32
YR = 48


def lanes_of(rows):
    return lax.broadcasted_iota(jnp.int32, (rows, LANES), 1)


def flag(value, rows):
    return jnp.broadcast_to(value, (rows, LANES)) == 1


def roll(v, by, axis=1):
    size = v.shape[axis]
    by = by % size
    return v if by == 0 else pltpu.roll(v, by, axis)


def along(values, dim, func):
    out = [None] * 27
    step = (9, 3, 1)[dim]
    for base in range(27):
        if (base // step) % 3 == 0:
            a, b, c = func(values[base], values[base + step], values[base + 2 * step])
            out[base], out[base + step], out[base + 2 * step] = a, b, c
    return out


def to_moments(low, mid, high):
    both = low + high
    return both + 4.0 * mid, high - low, both


def from_moments(m0, m1, m2):
    return m2 - m1, m0 - 0.5 * m2, m1 + m2


def pack_x(load, put):
    for way in range(2):
        for half in range(2):
            put(way * 18 + half * 9, 9, load(0, way, None, half * HALF + (15 if way == 0 else 0)))


def pack_y(load, put):
    lane = lanes_of(HALF)
    last = None
    for way in range(2):
        slab = None
        for p in range(9):
            v = load(1, way, p, HALF if way == 0 else 0, HALF)
            source = 7 if way == 0 else 0
            slot = p if p < 8 else way
            v = roll(v, 16 * (slot - source))
            if p < 8:
                slab = v if slab is None else jnp.where(lane // 16 == slot, v, slab)
            else:
                last = v if last is None else jnp.where(lane // 16 == slot, v, last)
        put(way * HALF, HALF, slab)
    put(2 * HALF, HALF, last)


def pack_z(load, put):
    lane = lanes_of(ROWS) % 16
    for way in range(2):
        slab = None
        for p in range(9):
            v = roll(load(2, way, p, 0, ROWS), p - (15 if way == 0 else 0))
            slab = v if slab is None else jnp.where(lane == p, v, slab)
        put(way, slab)


def slab_face(ref, at, way, p, start):
    if p < 8:
        return roll(ref[at, pl.ds(way * HALF, HALF), :], start - 16 * p)
    return roll(ref[at, pl.ds(2 * HALF, HALF), :], start - 16 * way)


def kernel(
    levels,
    neighbours,
    rates,
    diffusivity,
    stoichiometry,
    pop,
    sca,
    old,
    new,
    out_pop,
    out_sca,
    ret_x,
    ret_y,
    ret_z,
    state,
    first,
    up0,
    up1,
    spec,
    spec2,
    lhs,
    res,
    bx_0,
    bx_1,
    by_0,
    by_1,
    bz_out_0,
    bz_out_1,
    bz_0,
    bz_1,
    sxy_0,
    sxy_1,
    sz_out_0,
    sz_out_1,
    sz_0,
    sz_1,
    rxy,
    rz_out,
    rz,
    send_sem,
    recv_sem,
):
    slots = pop.shape[0]
    devices = lax.axis_size("blk")
    me = lax.axis_index("blk")
    layers = devices // 2
    layer = me // 2
    core = me % 2
    partner = 2 * layer + 1 - core
    above = lax.rem(layer + 1, layers)
    below = lax.rem(layer + layers - 1, layers)
    mine = core * slots
    around = 2 * slots
    mesh_targets = ((2 * above, 2 * above + 1), (2 * below, 2 * below + 1))

    barrier = pltpu.get_barrier_semaphore()
    for device in (partner,) + mesh_targets[0] + mesh_targets[1]:
        pl.semaphore_signal(barrier, inc=1, device_id=(device,), device_id_type=MESH)

    counter = [0, 0]

    def send_partner(ref):
        s, r = counter[0], counter[1]
        counter[0] += 1
        counter[1] += 1
        part = ref.at[pl.ds(mine, slots)]
        copy = pltpu.make_async_remote_copy(
            src_ref=part,
            dst_ref=part,
            send_sem=send_sem.at[s],
            recv_sem=recv_sem.at[r],
            device_id=(partner,),
            device_id_type=MESH,
        )
        copy.start()
        other = ref.at[pl.ds(slots - mine, slots)]
        arrival = pltpu.make_async_remote_copy(
            src_ref=other,
            dst_ref=other,
            send_sem=send_sem.at[s],
            recv_sem=recv_sem.at[r],
            device_id=(partner,),
            device_id_type=MESH,
        )

        def wait():
            arrival.wait_recv()
            copy.wait_send()

        return wait

    def send_layers(source, target):
        waits = []
        for way in range(2):
            r = counter[1]
            counter[1] += 2
            for core_to in range(2):
                s = counter[0]
                counter[0] += 1
                copy = pltpu.make_async_remote_copy(
                    src_ref=source.at[way],
                    dst_ref=target.at[way, pl.ds(mine, slots)],
                    send_sem=send_sem.at[s],
                    recv_sem=recv_sem.at[r + core],
                    device_id=(mesh_targets[way][core_to],),
                    device_id_type=MESH,
                )
                copy.start()
                waits.append(copy.wait_send)
                arrival = pltpu.make_async_remote_copy(
                    src_ref=source.at[way],
                    dst_ref=target.at[way, pl.ds(core_to * slots, slots)],
                    send_sem=send_sem.at[s],
                    recv_sem=recv_sem.at[r + core_to],
                    device_id=(mesh_targets[way][core_to],),
                    device_id_type=MESH,
                )
                waits.append(arrival.wait_recv)

        def wait():
            for w in waits:
                w()

        return wait

    def each_block(body):
        def wrapped(b, carry):
            body(b)
            return carry

        lax.fori_loop(0, slots, wrapped, 0)

    def fine_of(b):
        return levels[me * slots + b]

    def place(b, q):
        return lax.rem(neighbours[b, q], around)

    def unpack_in(b):
        def one(x, carry):
            for half in range(2):
                column = pl.ds(pl.multiple_of((2 * x + half) * LANES, LANES), LANES)
                row = half * HALF + x
                state[b, pl.ds(row, 27, stride=ROWS), :] = pop[b, :, column]
                spec[b, pl.ds(row, 9, stride=ROWS), :] = sca[b, :, column]
            return carry

        lax.fori_loop(0, HALF, one, 0)

    each_block(unpack_in)

    def spread_coarse(target, average):
        lhs[...] = jnp.zeros(lhs.shape, F32)
        for b in range(slots):
            for chunk in range(4):
                v = old[b, :, pl.ds(chunk * LANES, LANES)]
                if average:
                    v = 0.5 * (v + new[b, :, pl.ds(chunk * LANES, LANES)])
                lhs[pl.ds((b * 4 + chunk) * ROWS, 27), :] = v
        a = lhs[...]
        a0 = a.astype(jnp.bfloat16)
        rest = a - a0.astype(F32)
        a1 = rest.astype(jnp.bfloat16)
        a2 = (rest - a1.astype(F32)).astype(jnp.bfloat16)
        row = lax.broadcasted_iota(jnp.int32, (LANES, LANES), 0)
        col = lax.broadcasted_iota(jnp.int32, (LANES, LANES), 1)
        want = (col // 32) * 8 + (col % 16) // 2
        for variant in range(4):
            parity, half = variant // 2, variant % 2
            pick = jnp.where(row == want + parity * 64 + half * 32, 1.0, 0.0).astype(jnp.bfloat16)
            total = jnp.dot(a0, pick, preferred_element_type=F32)
            total = total + jnp.dot(a1, pick, preferred_element_type=F32)
            total = total + jnp.dot(a2, pick, preferred_element_type=F32)
            res[...] = total

            def scatter(g, carry):
                v = res[pl.ds(pl.multiple_of(g * ROWS, ROWS), 27), :]
                b = g // 4
                x = 2 * (2 * (g % 4) + parity)
                target[b, pl.ds(half * HALF + x, 27, stride=ROWS), :] = v
                target[b, pl.ds(half * HALF + x + 1, 27, stride=ROWS), :] = v
                return carry

            lax.fori_loop(0, slots * 4, scatter, 0)

    spread_coarse(up0, False)
    spread_coarse(up1, True)

    def population_load(b, spread):
        fine = fine_of(b)

        def load(dim, way, p, start, size=None):
            movers = MOVERS[dim][way]
            if p is None:
                at = pl.ds(ROWS * movers[0] + start, 9, stride=ROWS)
                return jnp.where(flag(fine, 9), state[b, at, :], spread[b, at, :])
            at = pl.ds(ROWS * movers[p] + start, size)
            return jnp.where(flag(fine, size), state[b, at, :], spread[b, at, :])

        return load

    def return_load(b):
        fine = fine_of(b)

        def load(dim, way, p, start, size=None):
            movers = MOVERS[dim][way]
            if p is None:
                at = pl.ds(ROWS * movers[0] + start, 9, stride=ROWS)
                rows = 9
            else:
                at = pl.ds(ROWS * movers[p] + start, size)
                rows = size
            return jnp.where(flag(fine, rows), 0.5 * first[b, at, :] + 0.5 * state[b, at, :], 0.0)

        return load

    def scalar_load(b, source):
        def load(dim, way, p, start, size=None):
            if p is None:
                return source[b, pl.ds(start, 9, stride=ROWS), :]
            return source[b, pl.ds(ROWS * p + start, size), :]

        return load

    def putter(ref, at, base=0):
        def put(start, size, value):
            ref[at, pl.ds(base + start, size), :] = value

        return put

    def putter_z(ref, b):
        def put(way, value):
            ref[way, b] = value

        return put

    def collide(keep):
        scale = [rates[k] * (3.375 / 216.0 * 2.0 ** sum(1 for d in (9, 3, 1) if (k // d) % 3)) for k in range(27)]

        def one(t, carry):
            b = t // 4
            base = pl.multiple_of((t % 4) * 8, 8)

            def at(i):
                return pl.ds(base + ROWS * i, 8)

            g = [state[b, at(i), :] for i in range(27)]
            m = along(along(along(g, 2, to_moments), 1, to_moments), 0, to_moments)
            rho = m[0]
            jx, jy, jz = m[9], m[3], m[1]
            unit = 1.0 / 216.0
            hx, hy, hz = jx * unit, jy * unit, jz * unit
            third = 1.0 / 3.0
            qx, qy, qz = jx * hx, jy * hy, jz * hz
            eq = [None] * 27
            eq[0] = rho
            eq[9], eq[3], eq[1] = jx, jy, jz
            rho3 = rho * third
            eq[18], eq[6], eq[2] = rho3 + qx, rho3 + qy, rho3 + qz
            xy, xz, yz = jx * hy, jx * hz, jy * hz
            eq[12], eq[10], eq[4] = xy, xz, yz
            jx3, jy3, jz3 = jx * third, jy * third, jz * third
            eq[21], eq[19] = jy3, jz3
            eq[15], eq[7] = jx3, jz3
            eq[11], eq[5] = jx3, jy3
            rho9 = rho3 * third
            qx3, qy3, qz3 = qx * third, qy * third, qz * third
            eq[24] = rho9 + qx3 + qy3
            eq[20] = rho9 + qx3 + qz3
            eq[8] = rho9 + qy3 + qz3
            eq[22], eq[16], eq[14] = yz * third, xz * third, xy * third
            eq[25], eq[23], eq[17] = jz3 * third, jy3 * third, jx3 * third
            eq[26] = (rho9 + qx3 + qy3 + qz3) * third
            delta = [
                scale[k] * (m[k] if eq[k] is None else m[k] - eq[k]) for k in range(27)
            ]
            back = along(along(along(delta, 0, from_moments), 1, from_moments), 2, from_moments)
            for i in range(27):
                post = state[b, at(i), :] - back[i]
                state[b, at(i), :] = post
                if keep:
                    first[b, at(i), :] = post
            return carry

        lax.fori_loop(0, slots * 4, one, 0)

    def section_x(recv):
        def body(b):
            for p in range(9):
                for half in range(2):
                    up = ROWS * MOVERS[0][0][p] + half * HALF
                    down = ROWS * MOVERS[0][1][p] + half * HALF
                    v = state[b, pl.ds(up, 15), :]
                    w = state[b, pl.ds(down + 1, 15), :]
                    state[b, pl.ds(up + 1, 15), :] = v
                    state[b, pl.ds(down, 15), :] = w
            low, high = place(b, 0), place(b, 1)
            for half in range(2):
                state[b, pl.ds(ROWS * 18 + half * HALF, 9, stride=ROWS), :] = recv[
                    low, pl.ds(half * 9, 9), :
                ]
                state[b, pl.ds(half * HALF + 15, 9, stride=ROWS), :] = recv[
                    high, pl.ds(18 + half * 9, 9), :
                ]

        each_block(body)

    def section_y(recv):
        def body(b):
            lane = lanes_of(HALF)
            low, high = place(b, 2), place(b, 3)
            for p in range(9):
                i = MOVERS[1][0][p]
                e = roll(state[b, pl.ds(ROWS * i, HALF), :], 16)
                o = roll(state[b, pl.ds(ROWS * i + HALF, HALF), :], 16)
                state[b, pl.ds(ROWS * i + HALF, HALF), :] = jnp.where(lane < 16, e, o)
                state[b, pl.ds(ROWS * i, HALF), :] = jnp.where(
                    lane < 16, slab_face(recv, low, 0, p, 0), e
                )
                i = MOVERS[1][1][p]
                e = roll(state[b, pl.ds(ROWS * i, HALF), :], -16)
                o = roll(state[b, pl.ds(ROWS * i + HALF, HALF), :], -16)
                state[b, pl.ds(ROWS * i, HALF), :] = jnp.where(lane >= 112, o, e)
                state[b, pl.ds(ROWS * i + HALF, HALF), :] = jnp.where(
                    lane >= 112, slab_face(recv, high, 1, p, 112), o
                )

        each_block(body)

    def section_z(recv):
        def body(b):
            lane = lanes_of(ROWS) % 16
            low = recv[0, place(b, 4)]
            high = recv[1, place(b, 5)]
            for p in range(9):
                at = pl.ds(ROWS * MOVERS[2][0][p], ROWS)
                state[b, at, :] = jnp.where(lane == 0, roll(low, -p), roll(state[b, at, :], 1))
                at = pl.ds(ROWS * MOVERS[2][1][p], ROWS)
                state[b, at, :] = jnp.where(
                    lane == 15, roll(high, 15 - p), roll(state[b, at, :], -1)
                )

        each_block(body)

    def advance(source, target, recv, recv_z):
        def body(b):
            row = lax.broadcasted_iota(jnp.int32, (HALF, LANES), 0)
            lane = lanes_of(HALF)
            near = lane % 16
            known = [flag(levels[neighbours[b, q]], HALF) for q in range(6)]
            spot = [place(b, q) for q in range(6)]
            e8 = [source[b, pl.ds(ROWS * 8 + h * HALF, HALF), :] for h in range(2)]
            burn = [
                source[b, pl.ds(h * HALF, HALF), :]
                * source[b, pl.ds(ROWS + h * HALF, HALF), :]
                * jnp.exp(4.0 * (e8[h] - 1.0))
                for h in range(2)
            ]
            drift = []
            for half in range(2):

                def get(i):
                    return state[b, pl.ds(ROWS * i + half * HALF, HALF), :]

                g = [get(i) for i in range(27)]
                weighted = lambda a, c, f: (a + f) * (1.0 / 6.0) + c * (2.0 / 3.0)
                slope = lambda a, f: (f - a) * (1.0 / 6.0)
                zsum = [weighted(g[3 * k], g[3 * k + 1], g[3 * k + 2]) for k in range(9)]
                zdif = [slope(g[3 * k], g[3 * k + 2]) for k in range(9)]
                ysum = [weighted(zsum[3 * k], zsum[3 * k + 1], zsum[3 * k + 2]) for k in range(3)]
                ydif = [slope(zsum[3 * k], zsum[3 * k + 2]) for k in range(3)]
                zrow = [weighted(zdif[3 * k], zdif[3 * k + 1], zdif[3 * k + 2]) for k in range(3)]
                drift.append((slope(ysum[0], ysum[2]), weighted(*ydif), weighted(*zrow)))
            for m in range(9):
                e = source[b, pl.ds(ROWS * m, HALF), :]
                o = source[b, pl.ds(ROWS * m + HALF, HALF), :]
                pair = (e, o)
                up_y, down_y = roll(e, -16), roll(o, -16)
                up_y = (
                    jnp.where(lane >= 112, down_y, up_y),
                    jnp.where(
                        lane >= 112,
                        jnp.where(known[3], slab_face(recv.at[:, pl.ds(XR, YR)], spot[3], 1, m, 112), o),
                        down_y,
                    ),
                )
                re, ro = roll(e, 16), roll(o, 16)
                down_y = (
                    jnp.where(
                        lane < 16,
                        jnp.where(known[2], slab_face(recv.at[:, pl.ds(XR, YR)], spot[2], 0, m, 0), e),
                        re,
                    ),
                    jnp.where(lane < 16, re, ro),
                )
                for half in range(2):
                    v = pair[half]
                    line = recv[spot[0], pl.ds(half * 9 + m, 1), :]
                    face = jnp.where(known[0], jnp.broadcast_to(line, v.shape), v)
                    down_x = jnp.where(row == 0, face, roll(v, 1, 0))
                    line = recv[spot[1], pl.ds(18 + half * 9 + m, 1), :]
                    face = jnp.where(known[1], jnp.broadcast_to(line, v.shape), v)
                    up_x = jnp.where(row == 15, face, roll(v, -1, 0))
                    face = roll(recv_z[0, spot[4], pl.ds(half * HALF, HALF), :], -m)
                    down_z = jnp.where(near == 0, jnp.where(known[4], face, v), roll(v, 1))
                    face = roll(recv_z[1, spot[5], pl.ds(half * HALF, HALF), :], 15 - m)
                    up_z = jnp.where(near == 15, jnp.where(known[5], face, v), roll(v, -1))
                    jx, jy, jz = drift[half]
                    moved = (
                        jx * (up_x - down_x)
                        + jy * (up_y[half] - down_y[half])
                        + jz * (up_z - down_z)
                    )
                    spread = (up_x + down_x) + (up_y[half] + down_y[half]) + (up_z + down_z) - 6.0 * v
                    target[b, pl.ds(ROWS * m + half * HALF, HALF), :] = (
                        v - 0.5 * moved + diffusivity[m] * spread + stoichiometry[m] * burn[half]
                    )

        each_block(body)

    pl.semaphore_wait(barrier, 5)
    last_wait = None
    for substep in range(2):
        spread = (up0, up1)[substep]
        source, target = (spec, spec2) if substep == 0 else (spec2, spec)
        cx, cy, cz_out, cz = ((bx_0, by_0, bz_out_0, bz_0), (bx_1, by_1, bz_out_1, bz_1))[substep]
        cs, cs_out, cs_z = ((sxy_0, sz_out_0, sz_0), (sxy_1, sz_out_1, sz_1))[substep]

        def pack_scalars(b):
            load = scalar_load(b, source)
            pack_x(load, putter(cs, mine + b))
            pack_y(load, putter(cs, mine + b, XR))
            pack_z(load, putter_z(cs_out, b))

        each_block(pack_scalars)
        wait_s = send_partner(cs)
        wait_sz = send_layers(cs_out, cs_z)
        collide(substep == 0)
        each_block(lambda b: pack_x(population_load(b, spread), putter(cx, mine + b)))
        wait = send_partner(cx)
        if substep == 1:

            def pack_return(b):
                load = return_load(b)
                pack_x(load, putter(rxy, mine + b))
                pack_y(load, putter(rxy, mine + b, XR))
                pack_z(load, putter_z(rz_out, b))

            each_block(pack_return)
            wait_r = send_partner(rxy)
            wait_rz = send_layers(rz_out, rz)
        wait()
        section_x(cx)
        each_block(lambda b: pack_y(population_load(b, spread), putter(cy, mine + b)))
        send_partner(cy)()
        section_y(cy)
        each_block(lambda b: pack_z(population_load(b, spread), putter_z(cz_out, b)))
        wait = send_layers(cz_out, cz)
        wait()
        section_z(cz)
        wait_s()
        wait_sz()
        advance(source, target, cs, cs_z)
    wait_r()
    wait_rz()

    def pack_out(b):
        fine = fine_of(b)

        def one(x, carry):
            for half in range(2):
                column = pl.ds(pl.multiple_of((2 * x + half) * LANES, LANES), LANES)
                row = half * HALF + x
                out_pop[b, :, column] = jnp.where(
                    flag(fine, 27), state[b, pl.ds(row, 27, stride=ROWS), :], pop[b, :, column]
                )
                out_sca[b, :, column] = jnp.where(
                    flag(fine, 9), spec[b, pl.ds(row, 9, stride=ROWS), :], sca[b, :, column]
                )
            return carry

        lax.fori_loop(0, HALF, one, 0)
        for way in range(2):
            ret_x[b, way] = rxy[place(b, way), pl.ds(18 * way, 18), :]
            at = place(b, 2 + way)
            ret_y[b, way, pl.ds(0, HALF), :] = rxy[at, pl.ds(XR + HALF * way, HALF), :]
            ret_y[b, way, pl.ds(HALF, HALF), :] = rxy[at, pl.ds(XR + 2 * HALF, HALF), :]
            ret_z[b, way] = rz[way, place(b, 4 + way)]

    each_block(pack_out)


def local(
    populations,
    scalars,
    coarse_old,
    coarse_new,
    levels,
    neighbours,
    relax_rates,
    diffusivity,
    stoichiometry,
):
    slots = populations.shape[0]
    vmem = pl.BlockSpec(memory_space=pltpu.VMEM)
    smem = pl.BlockSpec(memory_space=pltpu.SMEM)
    shape = jax.ShapeDtypeStruct
    layer = 2 * slots
    outs = pl.pallas_call(
        kernel,
        out_shape=(
            shape(populations.shape, F32),
            shape(scalars.shape, F32),
            shape((slots, 2, 18, LANES), F32),
            shape((slots, 2, 32, LANES), F32),
            shape((slots, 2, 32, LANES), F32),
        ),
        in_specs=[smem] * 5 + [vmem] * 4,
        out_specs=[vmem] * 5,
        scratch_shapes=[
            pltpu.VMEM((slots, POP_ROWS, LANES), F32),
            pltpu.VMEM((slots, POP_ROWS, LANES), F32),
            pltpu.VMEM((slots, POP_ROWS, LANES), F32),
            pltpu.VMEM((slots, POP_ROWS, LANES), F32),
            pltpu.VMEM((slots, SCA_ROWS, LANES), F32),
            pltpu.VMEM((slots, SCA_ROWS, LANES), F32),
            pltpu.VMEM((slots * 4 * ROWS, LANES), F32),
            pltpu.VMEM((slots * 4 * ROWS, LANES), F32),
            pltpu.VMEM((layer + 1, XR, LANES), F32),
            pltpu.VMEM((layer + 1, XR, LANES), F32),
            pltpu.VMEM((layer, YR, LANES), F32),
            pltpu.VMEM((layer, YR, LANES), F32),
            pltpu.VMEM((2, slots, ROWS, LANES), F32),
            pltpu.VMEM((2, slots, ROWS, LANES), F32),
            pltpu.VMEM((2, layer, ROWS, LANES), F32),
            pltpu.VMEM((2, layer, ROWS, LANES), F32),
            pltpu.VMEM((layer, XR + YR, LANES), F32),
            pltpu.VMEM((layer, XR + YR, LANES), F32),
            pltpu.VMEM((2, slots, ROWS, LANES), F32),
            pltpu.VMEM((2, slots, ROWS, LANES), F32),
            pltpu.VMEM((2, layer, ROWS, LANES), F32),
            pltpu.VMEM((2, layer, ROWS, LANES), F32),
            pltpu.VMEM((layer, XR + YR, LANES), F32),
            pltpu.VMEM((2, slots, ROWS, LANES), F32),
            pltpu.VMEM((2, layer, ROWS, LANES), F32),
            pltpu.SemaphoreType.DMA((32,)),
            pltpu.SemaphoreType.DMA((32,)),
        ],
        compiler_params=pltpu.CompilerParams(
            collective_id=0, has_side_effects=True, vmem_limit_bytes=56 << 20
        ),
    )(
        levels,
        neighbours,
        relax_rates,
        diffusivity,
        stoichiometry,
        populations,
        scalars,
        coarse_old,
        coarse_new,
    )
    new_populations, new_scalars, ret_x, ret_y, ret_z = outs
    x = ret_x.reshape(slots, 2, 2, 9, 4, 2, 8, 2).sum(axis=(5, 7))
    x = x.transpose(0, 1, 3, 2, 4, 5).reshape(slots, 2, 9, 64)
    y = ret_y.reshape(slots, 2, 2, 8, 2, 8, 8, 2).sum(axis=(4, 7))
    y8 = jnp.stack([y[:, 0, 1, :, 0], y[:, 1, 1, :, 1]], axis=1)
    y = jnp.concatenate([y[:, :, 0], y8[:, :, :, None]], axis=3)
    y = y.transpose(0, 1, 3, 2, 4).reshape(slots, 2, 9, 64)
    z = ret_z.reshape(slots, 2, 2, 8, 2, 4, 2, 16).sum(axis=(4, 6))[..., :9]
    z = z.transpose(0, 1, 5, 3, 2, 4).reshape(slots, 2, 9, 64)
    own = lax.dynamic_slice_in_dim(levels, lax.axis_index("blk") * slots, slots)
    back = 0.25 * jnp.concatenate([x, y, z], axis=1).reshape(slots, -1)
    back = jnp.where((own == 1)[:, None], 0.0, back)
    return new_populations, new_scalars, back


def solution(mesh):
    in_specs = (
        P("blk", None, None),
        P("blk", None, None),
        P("blk", None, None),
        P("blk", None, None),
        P(),
        P("blk", None),
        P(),
        P(),
        P(),
    )
    out_specs = (P("blk", None, None), P("blk", None, None), P("blk", None))
    return jax.shard_map(local, mesh=mesh, in_specs=in_specs, out_specs=out_specs, check_vma=False)
```

time: 567 us -> 85.9 us (0.15); the launches traced: 558 us -> 85.3 us
  local copies, waits for them, and re-layouts: 357 us -> 21.4 us
  other arithmetic: 90.2 us -> 9.44 us
  starting transfers between devices: 70.2 us -> 0 us
  Pallas kernels: 0 us -> 53.7 us
  matrix products: 22.8 us -> 0 us
  waiting for transfers between devices: 14.5 us -> 0 us
    another operation x85 -> x1, local copies, waits for them, and re-layouts: 107 us -> 0.01 us  [local(): y8 = jnp.stack([y[:, 0, 1, :, 0], y[:, 1, 1, :, 1]], axis=1)]
    slice x87 -> x0, local copies, waits for them, and re-layouts: 96.1 us -> none  [the longest x20 39.2 us: layer_of(): lax.slice_in_dim(flat, index, flat.shape[-1], stride=extent, axis=last_axis)]
    ppermute x44 -> x0, starting transfers between devices: 70.2 us -> none  [shifted_2(): lax.ppermute(shard, axis, [(i, (i + by) % devices) for i in range(devices)])]
    pallas_call x0 -> x1, Pallas kernels: none -> 53.7 us  [local(): pl.pallas_call(kernel, out_shape=(shape(populations.shape, F32), shape(sc...]
    reshape x22 -> x5, local copies, waits for them, and re-layouts: 46.7 us -> 2.47 us  [the longest x1 1.36 us: local(): z = ret_z.reshape(slots, 2, 2, 8, 2, 4, 2, 16).sum(axis=(4, 6))[..., :9]]
    gather x51 -> x0, local copies, waits for them, and re-layouts: 39.7 us -> none  [the longest x20 22.2 us: side_values(): nearby[distance[:, facing] + base, positions[:, facing], facing ^ 1]]
    another operation x41 -> x0, other arithmetic: 32.4 us -> none  [the longest x23 18.2 us: collect(): return jnp.stack(pieces, axis=0)]
    broadcast_in_dim x33 -> x1, local copies, waits for them, and re-layouts: 32.8 us -> 1.02 us  [local(): y = jnp.concatenate([y[:, :, 0], y8[:, :, :, None]], axis=3)]
  transfers between devices with their start and end apart: 44 -> 0, of which waited for: 8 -> 0; matrix products, arithmetic and copies ran while one was open for 67% -> 0% of each run, Pallas kernels for 0% -> 0%
where the time goes in v1:
time: 85.9 us; the launch traced here: 85.3 us
  Pallas kernels  53.7 us (63%)
  local copies, waits for them, and re-layouts  21.4 us (25%)
  other arithmetic  9.44 us (11%)
    pallas_call x1, Pallas kernels, local(): pl.pallas_call(kernel, out_shape=(shape(populations.shape, F32), shape(sc...  53.7 us
    unnamed x16, local copies, waits for them, and re-layouts  13.4 us
    reduce_sum x1, other arithmetic, local(): y = ret_y.reshape(slots, 2, 2, 8, 2, 8, 8, 2).sum(axis=(4, 7))  5.6 us
    pallas_call x2, local copies, waits for them, and re-layouts, local(): pl.pallas_call(kernel, out_shape=(shape(populations.shape, F32), shape(sc...  2.83 us

profile of v1, /device:TPU:0, one launch (start us, length us, event | category | flops | bytes accessed | tf_op | source)
XLA Modules:
  0.0 85.3 jit_solution(14753523307996280110)
XLA Ops:
  0.6 0.0 copy-start
  0.6 0.9 %dynamic-slice_compare_fusion = pred[4]{0:T(512)(128)(4,1)S(1)} fusion(s32[128]{0:T(128)} %levels.1, s32[]{:T(128)S(6)} %select_n.7), kind=kLoop, calls=%fused_computation.8 | loop fusion | flops 4 | bytes 24 | tf_op jit(solution)/shard_map/eq | solution.py:676
  1.5 1.7 %copy.49.old = f32[4,27,512]{2,1,0:T(8,128)} copy(f32[4,27,512]{2,0,1:T(4,128)} %param.11) | data formatting | bytes 442368 | tf_op args[2]
  3.2 1.7 %copy.50.new = f32[4,27,512]{2,1,0:T(8,128)} copy(f32[4,27,512]{2,0,1:T(4,128)} %param.12) | data formatting | bytes 442368 | tf_op args[3]
  4.9 2.4 %copy.48.sca = f32[4,9,4096]{2,1,0:T(8,128)} copy(f32[4,9,4096]{2,0,1:T(4,128)} %param.10) | data formatting | bytes 1179648 | tf_op args[1]
  7.3 0.0 copy-done
  7.3 2.4 %copy.47.pop = f32[4,27,4096]{2,1,0:T(8,128)} copy(f32[4,27,4096]{2,0,1:T(4,128)S(1)} %copy-done) | data formatting | bytes 3538944 | tf_op args[0]
  9.7 53.7 %shard_map.112 = (f32[4,27,4096]{2,1,0:T(8,128)}, f32[4,9,4096]{2,1,0:T(8,128)}, f32[4,2,18,128]{3,2,1,0:T(8,128)}, f32[4,2,32,128]{3,2,1,0:T(8,128)}, f32[4,2,32,128]{3,2,1,0:T(8,128)}) custom-call(s32[128]{0:T(128)} %levels.1, s32[4,6]{1,0:T(4,128)} %neighbours.1, f32[27]{0:T(128)} %rates.1, f32[9]{0:T(128)} %diffusivity.1, f32[9]{0:T(128)} %stoichiometry.1, ...), custom_call_target="tpu_custom_call" | custom-call | tf_op jit(solution)/shard_map/pallas_call | solution.py:611
  63.4 0.0 copy-start.4
  63.4 4.0 %copy.61 = f32[4,27,4096]{2,0,1:T(4,128)} copy(f32[4,27,4096]{2,1,0:T(8,128)} %get-tuple-element.22) | data formatting | bytes 3538944
  67.4 0.0 copy-done.4
  67.4 0.0 copy-start.1
  67.4 0.2 copy.51
  67.6 0.6 reshape.28
  68.2 0.0 copy-start.3
  68.2 0.8 reduce_sum.27
  69.0 0.5 copy.52
  69.5 0.2 reshape.29
  69.7 0.0 copy-done.1
  69.7 1.2 %copy.62 = f32[4,9,4096]{2,0,1:T(4,128)} copy(f32[4,9,4096]{2,1,0:T(8,128)S(1)} %copy-done.1) | data formatting | bytes 1179648
  70.9 0.0 copy-done.3
  70.9 0.0 copy-start.2
  70.9 1.4 %reshape.32 = f32[4,2,2,8,2,4,2,16]{7,6,5,4,3,2,1,0:T(2,128)S(1)} reshape(f32[4,2,32,128]{3,2,1,0:T(8,128)S(1)} %copy-done.3) | data formatting | bytes 262144 | tf_op jit(solution)/shard_map/reshape | solution.py:672
  72.3 1.3 %reduce_sum.29 = f32[4,2,2,8,4,16]{5,4,3,2,1,0:T(4,128)S(1)} reduce(f32[4,2,2,8,2,4,2,16]{7,6,5,4,3,2,1,0:T(2,128)S(1)} %reshape.32, f32[]{:T(128)} %constant.5.clone.1), dimensions={4,6}, to_apply=%region_2.0 | reduce | flops 24576 | bytes 163844 | tf_op jit(solution)/shard_map/reduce_sum | solution.py:672
  73.6 0.1 copy.59
  73.8 0.0 copy-done.2
  73.8 2.6 %copy.53 = f32[4,2,32,128]{0,3,2,1:T(8,128)} copy(f32[4,2,32,128]{3,2,1,0:T(8,128)S(1)} %copy-done.2) | data formatting | bytes 262144 | tf_op jit(solution)/shard_map/pallas_call | solution.py:611
  76.4 5.6 %reduce_sum.28 = f32[4,2,2,8,8,8]{0,5,4,3,2,1:T(8,128)S(1)} reduce(f32[4,2,2,8,2,8,8,2]{0,7,6,5,4,3,2,1:T(2,128)} %bitcast.27, f32[]{:T(128)} %constant.5.clone.1), dimensions={4,7}, to_apply=%region_1.0 | reduce | flops 24576 | bytes 163844 | tf_op jit(solution)/shard_map/reduce_sum | solution.py:668
  82.1 1.0 %copy.55 = f32[4,2,8,8,8]{3,4,2,1,0:T(8,128)S(1)} copy(f32[4,2,8,8,8]{0,4,3,2,1:T(8,128)S(1)} %slice_bitcast_fusion) | data formatting | bytes 32768 | tf_op jit(solution)/shard_map/squeeze | solution.py:670
  83.1 1.0 %copy.56 = f32[4,2,8,1,8]{3,4,2,1,0:T(8,128)S(1)} copy(f32[4,2,8,1,8]{0,4,2,1,3:T(8,128)S(1)} %maximum_bitcast_fusion.1) | data formatting | bytes 4096 | tf_op jit(solution)/shard_map/broadcast_in_dim | solution.py:670
  84.1 0.2 maximum_bitcast_fusion
  84.3 0.1 copy.63
  84.4 0.1 maximum_multiply_fusion
  84.5 0.1 mul.15
  84.6 0.7 broadcast_select_fusion
  (6 shorter events, 0.2 us)
Async XLA Ops:
  0.6 6.7 %copy-start = (f32[4,27,4096]{2,0,1:T(4,128)S(1)}, f32[4,27,4096]{2,0,1:T(4,128)}, u32[]{:S(2)}) copy-start(f32[4,27,4096]{2,0,1:T(4,128)} %param.9) | copy-start | bytes 5308420
  63.4 4.0 %copy-start.4 = (f32[4,2,18,128]{3,2,1,0:T(8,128)S(1)}, f32[4,2,18,128]{3,2,1,0:T(8,128)}, u32[]{:S(2)}) copy-start(f32[4,2,18,128]{3,2,1,0:T(8,128)} %get-tuple-element.10) | copy-start | bytes 221188
  67.4 2.3 %copy-start.1 = (f32[4,9,4096]{2,1,0:T(8,128)S(1)}, f32[4,9,4096]{2,1,0:T(8,128)}, u32[]{:S(2)}) copy-start(f32[4,9,4096]{2,1,0:T(8,128)} %get-tuple-element.23) | copy-start | bytes 1769476
  68.2 2.7 %copy-start.3 = (f32[4,2,32,128]{3,2,1,0:T(8,128)S(1)}, f32[4,2,32,128]{3,2,1,0:T(8,128)}, u32[]{:S(2)}) copy-start(f32[4,2,32,128]{3,2,1,0:T(8,128)} %get-tuple-element.12) | copy-start | bytes 393220
  70.9 2.9 %copy-start.2 = (f32[4,2,32,128]{3,2,1,0:T(8,128)S(1)}, f32[4,2,32,128]{3,2,1,0:T(8,128)}, u32[]{:S(2)}) copy-start(f32[4,2,32,128]{3,2,1,0:T(8,128)} %get-tuple-element.11) | copy-start | bytes 393220

commit v2 on v1

--- a/solution.py
+++ b/solution.py
@@ -57,6 +57,19 @@
 
 def from_moments(m0, m1, m2):
     return m2 - m1, m0 - 0.5 * m2, m1 + m2
+
+
+def split(a):
+    a0 = a.astype(jnp.bfloat16)
+    rest = a - a0.astype(F32)
+    a1 = rest.astype(jnp.bfloat16)
+    return a0, a1, (rest - a1.astype(F32)).astype(jnp.bfloat16)
+
+
+def product(parts, right):
+    total = jnp.dot(parts[2], right, preferred_element_type=F32)
+    total = total + jnp.dot(parts[1], right, preferred_element_type=F32)
+    return total + jnp.dot(parts[0], right, preferred_element_type=F32)
 
 
 def pack_x(load, put):
@@ -120,8 +133,8 @@
     up1,
     spec,
     spec2,
-    lhs,
     res,
+    slopes,
     bx_0,
     bx_1,
     by_0,
@@ -142,7 +155,7 @@
     send_sem,
     recv_sem,
 ):
-    slots = pop.shape[0]
+    slots = neighbours.shape[0]
     devices = lax.axis_size("blk")
     me = lax.axis_index("blk")
     layers = devices // 2
@@ -238,55 +251,40 @@
     def place(b, q):
         return lax.rem(neighbours[b, q], around)
 
+    def native(i, half, b):
+        return pl.ds(i * 2 * HALF * slots + half * slots + b, HALF, stride=2 * slots)
+
     def unpack_in(b):
-        def one(x, carry):
-            for half in range(2):
-                column = pl.ds(pl.multiple_of((2 * x + half) * LANES, LANES), LANES)
-                row = half * HALF + x
-                state[b, pl.ds(row, 27, stride=ROWS), :] = pop[b, :, column]
-                spec[b, pl.ds(row, 9, stride=ROWS), :] = sca[b, :, column]
-            return carry
-
-        lax.fori_loop(0, HALF, one, 0)
+        for half in range(2):
+            for i in range(27):
+                state[b, pl.ds(ROWS * i + half * HALF, HALF), :] = pop[native(i, half, b), :]
+            for m in range(9):
+                spec[b, pl.ds(ROWS * m + half * HALF, HALF), :] = sca[native(m, half, b), :]
 
     each_block(unpack_in)
 
     def spread_coarse(target, average):
-        lhs[...] = jnp.zeros(lhs.shape, F32)
-        for b in range(slots):
-            for chunk in range(4):
-                v = old[b, :, pl.ds(chunk * LANES, LANES)]
-                if average:
-                    v = 0.5 * (v + new[b, :, pl.ds(chunk * LANES, LANES)])
-                lhs[pl.ds((b * 4 + chunk) * ROWS, 27), :] = v
-        a = lhs[...]
-        a0 = a.astype(jnp.bfloat16)
-        rest = a - a0.astype(F32)
-        a1 = rest.astype(jnp.bfloat16)
-        a2 = (rest - a1.astype(F32)).astype(jnp.bfloat16)
+        a = 0.5 * (old[...] + new[...]) if average else old[...]
         row = lax.broadcasted_iota(jnp.int32, (LANES, LANES), 0)
         col = lax.broadcasted_iota(jnp.int32, (LANES, LANES), 1)
         want = (col // 32) * 8 + (col % 16) // 2
+        parts = split(a)
         for variant in range(4):
             parity, half = variant // 2, variant % 2
             pick = jnp.where(row == want + parity * 64 + half * 32, 1.0, 0.0).astype(jnp.bfloat16)
-            total = jnp.dot(a0, pick, preferred_element_type=F32)
-            total = total + jnp.dot(a1, pick, preferred_element_type=F32)
-            total = total + jnp.dot(a2, pick, preferred_element_type=F32)
-            res[...] = total
-
-            def scatter(g, carry):
-                v = res[pl.ds(pl.multiple_of(g * ROWS, ROWS), 27), :]
-                b = g // 4
-                x = 2 * (2 * (g % 4) + parity)
-                target[b, pl.ds(half * HALF + x, 27, stride=ROWS), :] = v
-                target[b, pl.ds(half * HALF + x + 1, 27, stride=ROWS), :] = v
+            res[pl.ds(0, a.shape[0]), :] = product(parts, pick)
+
+            def scatter(b, carry):
+                for chunk in range(4):
+                    v = res[pl.ds(chunk * slots + b, 27, stride=4 * slots), :]
+                    x = 2 * (2 * chunk + parity)
+                    target[b, pl.ds(half * HALF + x, 27, stride=ROWS), :] = v
+                    target[b, pl.ds(half * HALF + x + 1, 27, stride=ROWS), :] = v
                 return carry
 
-            lax.fori_loop(0, slots * 4, scatter, 0)
+            lax.fori_loop(0, slots, scatter, 0)
 
     spread_coarse(up0, False)
-    spread_coarse(up1, True)
 
     def population_load(b, spread):
         fine = fine_of(b)
@@ -386,65 +384,69 @@
 
         lax.fori_loop(0, slots * 4, one, 0)
 
-    def section_x(recv):
-        def body(b):
-            for p in range(9):
-                for half in range(2):
-                    up = ROWS * MOVERS[0][0][p] + half * HALF
-                    down = ROWS * MOVERS[0][1][p] + half * HALF
-                    v = state[b, pl.ds(up, 15), :]
-                    w = state[b, pl.ds(down + 1, 15), :]
-                    state[b, pl.ds(up + 1, 15), :] = v
-                    state[b, pl.ds(down, 15), :] = w
-            low, high = place(b, 0), place(b, 1)
+    def shift_x(b):
+        for p in range(9):
             for half in range(2):
-                state[b, pl.ds(ROWS * 18 + half * HALF, 9, stride=ROWS), :] = recv[
-                    low, pl.ds(half * 9, 9), :
-                ]
-                state[b, pl.ds(half * HALF + 15, 9, stride=ROWS), :] = recv[
-                    high, pl.ds(18 + half * 9, 9), :
-                ]
-
-        each_block(body)
-
-    def section_y(recv):
-        def body(b):
-            lane = lanes_of(HALF)
-            low, high = place(b, 2), place(b, 3)
-            for p in range(9):
-                i = MOVERS[1][0][p]
-                e = roll(state[b, pl.ds(ROWS * i, HALF), :], 16)
-                o = roll(state[b, pl.ds(ROWS * i + HALF, HALF), :], 16)
-                state[b, pl.ds(ROWS * i + HALF, HALF), :] = jnp.where(lane < 16, e, o)
-                state[b, pl.ds(ROWS * i, HALF), :] = jnp.where(
-                    lane < 16, slab_face(recv, low, 0, p, 0), e
-                )
-                i = MOVERS[1][1][p]
-                e = roll(state[b, pl.ds(ROWS * i, HALF), :], -16)
-                o = roll(state[b, pl.ds(ROWS * i + HALF, HALF), :], -16)
-                state[b, pl.ds(ROWS * i, HALF), :] = jnp.where(lane >= 112, o, e)
-                state[b, pl.ds(ROWS * i + HALF, HALF), :] = jnp.where(
-                    lane >= 112, slab_face(recv, high, 1, p, 112), o
-                )
-
-        each_block(body)
-
-    def section_z(recv):
-        def body(b):
-            lane = lanes_of(ROWS) % 16
-            low = recv[0, place(b, 4)]
-            high = recv[1, place(b, 5)]
-            for p in range(9):
-                at = pl.ds(ROWS * MOVERS[2][0][p], ROWS)
-                state[b, at, :] = jnp.where(lane == 0, roll(low, -p), roll(state[b, at, :], 1))
-                at = pl.ds(ROWS * MOVERS[2][1][p], ROWS)
-                state[b, at, :] = jnp.where(
-                    lane == 15, roll(high, 15 - p), roll(state[b, at, :], -1)
-                )
-
-        each_block(body)
-
-    def advance(source, target, recv, recv_z):
+                up = ROWS * MOVERS[0][0][p] + half * HALF
+                down = ROWS * MOVERS[0][1][p] + half * HALF
+                v = state[b, pl.ds(up, 15), :]
+                w = state[b, pl.ds(down + 1, 15), :]
+                state[b, pl.ds(up + 1, 15), :] = v
+                state[b, pl.ds(down, 15), :] = w
+
+    def enter_x(b, recv):
+        low, high = place(b, 0), place(b, 1)
+        for half in range(2):
+            state[b, pl.ds(ROWS * 18 + half * HALF, 9, stride=ROWS), :] = recv[
+                low, pl.ds(half * 9, 9), :
+            ]
+            state[b, pl.ds(half * HALF + 15, 9, stride=ROWS), :] = recv[
+                high, pl.ds(18 + half * 9, 9), :
+            ]
+
+    def shift_y(b):
+        lane = lanes_of(HALF)
+        for p in range(9):
+            even = pl.ds(ROWS * MOVERS[1][0][p], HALF)
+            odd = pl.ds(ROWS * MOVERS[1][0][p] + HALF, HALF)
+            e, o = roll(state[b, even, :], 16), roll(state[b, odd, :], 16)
+            state[b, odd, :] = jnp.where(lane < 16, e, o)
+            state[b, even, :] = e
+            even = pl.ds(ROWS * MOVERS[1][1][p], HALF)
+            odd = pl.ds(ROWS * MOVERS[1][1][p] + HALF, HALF)
+            e, o = roll(state[b, even, :], -16), roll(state[b, odd, :], -16)
+            state[b, even, :] = jnp.where(lane >= 112, o, e)
+            state[b, odd, :] = o
+
+    def enter_y(b, recv):
+        lane = lanes_of(HALF)
+        low, high = place(b, 2), place(b, 3)
+        for p in range(9):
+            at = pl.ds(ROWS * MOVERS[1][0][p], HALF)
+            state[b, at, :] = jnp.where(lane < 16, slab_face(recv, low, 0, p, 0), state[b, at, :])
+            at = pl.ds(ROWS * MOVERS[1][1][p] + HALF, HALF)
+            state[b, at, :] = jnp.where(
+                lane >= 112, slab_face(recv, high, 1, p, 112), state[b, at, :]
+            )
+
+    def shift_z(b):
+        for p in range(9):
+            at = pl.ds(ROWS * MOVERS[2][0][p], ROWS)
+            state[b, at, :] = roll(state[b, at, :], 1)
+            at = pl.ds(ROWS * MOVERS[2][1][p], ROWS)
+            state[b, at, :] = roll(state[b, at, :], -1)
+
+    def enter_z(b, recv):
+        lane = lanes_of(ROWS) % 16
+        low = recv[0, place(b, 4)]
+        high = recv[1, place(b, 5)]
+        for p in range(9):
+            at = pl.ds(ROWS * MOVERS[2][0][p], ROWS)
+            state[b, at, :] = jnp.where(lane == 0, roll(low, -p), state[b, at, :])
+            at = pl.ds(ROWS * MOVERS[2][1][p], ROWS)
+            state[b, at, :] = jnp.where(lane == 15, roll(high, 15 - p), state[b, at, :])
+
+    def prepare(source, target, recv, recv_z):
         def body(b):
             row = lax.broadcasted_iota(jnp.int32, (HALF, LANES), 0)
             lane = lanes_of(HALF)
@@ -458,21 +460,6 @@
                 * jnp.exp(4.0 * (e8[h] - 1.0))
                 for h in range(2)
             ]
-            drift = []
-            for half in range(2):
-
-                def get(i):
-                    return state[b, pl.ds(ROWS * i + half * HALF, HALF), :]
-
-                g = [get(i) for i in range(27)]
-                weighted = lambda a, c, f: (a + f) * (1.0 / 6.0) + c * (2.0 / 3.0)
-                slope = lambda a, f: (f - a) * (1.0 / 6.0)
-                zsum = [weighted(g[3 * k], g[3 * k + 1], g[3 * k + 2]) for k in range(9)]
-                zdif = [slope(g[3 * k], g[3 * k + 2]) for k in range(9)]
-                ysum = [weighted(zsum[3 * k], zsum[3 * k + 1], zsum[3 * k + 2]) for k in range(3)]
-                ydif = [slope(zsum[3 * k], zsum[3 * k + 2]) for k in range(3)]
-                zrow = [weighted(zdif[3 * k], zdif[3 * k + 1], zdif[3 * k + 2]) for k in range(3)]
-                drift.append((slope(ysum[0], ysum[2]), weighted(*ydif), weighted(*zrow)))
             for m in range(9):
                 e = source[b, pl.ds(ROWS * m, HALF), :]
                 o = source[b, pl.ds(ROWS * m + HALF, HALF), :]
@@ -507,15 +494,38 @@
                     down_z = jnp.where(near == 0, jnp.where(known[4], face, v), roll(v, 1))
                     face = roll(recv_z[1, spot[5], pl.ds(half * HALF, HALF), :], 15 - m)
                     up_z = jnp.where(near == 15, jnp.where(known[5], face, v), roll(v, -1))
+                    at = pl.ds(ROWS * m + half * HALF, HALF)
+                    slopes[0, b, at, :] = 0.5 * (up_x - down_x)
+                    slopes[1, b, at, :] = 0.5 * (up_y[half] - down_y[half])
+                    slopes[2, b, at, :] = 0.5 * (up_z - down_z)
+                    spread = (up_x + down_x) + (up_y[half] + down_y[half]) + (up_z + down_z) - 6.0 * v
+                    target[b, at, :] = v + diffusivity[m] * spread + stoichiometry[m] * burn[half]
+
+        each_block(body)
+
+    def finish(target):
+        def body(b):
+            drift = []
+            for half in range(2):
+
+                def get(i):
+                    return state[b, pl.ds(ROWS * i + half * HALF, HALF), :]
+
+                g = [get(i) for i in range(27)]
+                weighted = lambda a, c, f: (a + f) * (1.0 / 6.0) + c * (2.0 / 3.0)
+                slope = lambda a, f: (f - a) * (1.0 / 6.0)
+                zsum = [weighted(g[3 * k], g[3 * k + 1], g[3 * k + 2]) for k in range(9)]
+                zdif = [slope(g[3 * k], g[3 * k + 2]) for k in range(9)]
+                ysum = [weighted(zsum[3 * k], zsum[3 * k + 1], zsum[3 * k + 2]) for k in range(3)]
+                ydif = [slope(zsum[3 * k], zsum[3 * k + 2]) for k in range(3)]
+                zrow = [weighted(zdif[3 * k], zdif[3 * k + 1], zdif[3 * k + 2]) for k in range(3)]
+                drift.append((slope(ysum[0], ysum[2]), weighted(*ydif), weighted(*zrow)))
+            for m in range(9):
+                for half in range(2):
+                    at = pl.ds(ROWS * m + half * HALF, HALF)
                     jx, jy, jz = drift[half]
-                    moved = (
-                        jx * (up_x - down_x)
-                        + jy * (up_y[half] - down_y[half])
-                        + jz * (up_z - down_z)
-                    )
-                    spread = (up_x + down_x) + (up_y[half] + down_y[half]) + (up_z + down_z) - 6.0 * v
-                    target[b, pl.ds(ROWS * m + half * HALF, HALF), :] = (
-                        v - 0.5 * moved + diffusivity[m] * spread + stoichiometry[m] * burn[half]
+                    target[b, at, :] = target[b, at, :] - (
+                        jx * slopes[0, b, at, :] + jy * slopes[1, b, at, :] + jz * slopes[2, b, at, :]
                     )
 
         each_block(body)
@@ -534,9 +544,6 @@
             pack_y(load, putter(cs, mine + b, XR))
             pack_z(load, putter_z(cs_out, b))
 
-        each_block(pack_scalars)
-        wait_s = send_partner(cs)
-        wait_sz = send_layers(cs_out, cs_z)
         collide(substep == 0)
         each_block(lambda b: pack_x(population_load(b, spread), putter(cx, mine + b)))
         wait = send_partner(cx)
@@ -551,45 +558,145 @@
             each_block(pack_return)
             wait_r = send_partner(rxy)
             wait_rz = send_layers(rz_out, rz)
+        else:
+            each_block(pack_scalars)
+            wait_s = send_partner(cs)
+            wait_sz = send_layers(cs_out, cs_z)
+        each_block(shift_x)
         wait()
-        section_x(cx)
+        each_block(lambda b: enter_x(b, cx))
         each_block(lambda b: pack_y(population_load(b, spread), putter(cy, mine + b)))
-        send_partner(cy)()
-        section_y(cy)
+        wait = send_partner(cy)
+        if substep == 1:
+            each_block(pack_scalars)
+            wait_s = send_partner(cs)
+            wait_sz = send_layers(cs_out, cs_z)
+        else:
+            spread_coarse(up1, True)
+        each_block(shift_y)
+        wait()
+        each_block(lambda b: enter_y(b, cy))
         each_block(lambda b: pack_z(population_load(b, spread), putter_z(cz_out, b)))
         wait = send_layers(cz_out, cz)
-        wait()
-        section_z(cz)
+        each_block(shift_z)
         wait_s()
         wait_sz()
-        advance(source, target, cs, cs_z)
+        prepare(source, target, cs, cs_z)
+        wait()
+        each_block(lambda b: enter_z(b, cz))
+        finish(target)
     wait_r()
     wait_rz()
 
     def pack_out(b):
-        fine = fine_of(b)
-
-        def one(x, carry):
-            for half in range(2):
-                column = pl.ds(pl.multiple_of((2 * x + half) * LANES, LANES), LANES)
-                row = half * HALF + x
-                out_pop[b, :, column] = jnp.where(
-                    flag(fine, 27), state[b, pl.ds(row, 27, stride=ROWS), :], pop[b, :, column]
+        fine = flag(fine_of(b), HALF)
+        for half in range(2):
+            for i in range(27):
+                at = native(i, half, b)
+                out_pop[at, :] = jnp.where(
+                    fine, state[b, pl.ds(ROWS * i + half * HALF, HALF), :], pop[at, :]
                 )
-                out_sca[b, :, column] = jnp.where(
-                    flag(fine, 9), spec[b, pl.ds(row, 9, stride=ROWS), :], sca[b, :, column]
+            for m in range(9):
+                at = native(m, half, b)
+                out_sca[at, :] = jnp.where(
+                    fine, spec[b, pl.ds(ROWS * m + half * HALF, HALF), :], sca[at, :]
                 )
-            return carry
-
-        lax.fori_loop(0, HALF, one, 0)
         for way in range(2):
-            ret_x[b, way] = rxy[place(b, way), pl.ds(18 * way, 18), :]
+            at = place(b, way)
+            ret_x[0, b, way, pl.ds(0, 9), :] = rxy[at, pl.ds(18 * way, 9), :]
+            ret_x[1, b, way, pl.ds(0, 9), :] = rxy[at, pl.ds(18 * way + 9, 9), :]
             at = place(b, 2 + way)
             ret_y[b, way, pl.ds(0, HALF), :] = rxy[at, pl.ds(XR + HALF * way, HALF), :]
             ret_y[b, way, pl.ds(HALF, HALF), :] = rxy[at, pl.ds(XR + 2 * HALF, HALF), :]
             ret_z[b, way] = rz[way, place(b, 4 + way)]
 
     each_block(pack_out)
+
+
+def means_kernel(levels, ret_x, ret_y, ret_z, out, turned):
+    slots = out.shape[0]
+    first = lax.axis_index("blk") * slots
+    groups = slots // 2
+
+    def mask(b, rows):
+        return jnp.broadcast_to(levels[first + b], (rows, 64)) == 1
+
+    def grid(rows, columns):
+        return tuple(lax.broadcasted_iota(jnp.int32, (rows, columns), d) for d in range(2))
+
+    def pick(cond):
+        return jnp.where(cond, 0.25, 0.0).astype(jnp.bfloat16)
+
+    k, n = grid(LANES, 64)
+    total = None
+    for half in range(2):
+        right = pick(n == half * 32 + (k // 32) * 8 + (k % 16) // 2)
+        v = ret_x[half].reshape(slots * 2 * 16, LANES)
+        part = product(split(v), right)
+        total = part if total is None else total + part
+    for b in range(slots):
+        for way in range(2):
+            v = total[(b * 2 + way) * 16 : (b * 2 + way) * 16 + 9]
+            out[b, way] = jnp.where(mask(b, 9), 0.0, v)
+
+    k, n = grid(LANES, 512)
+    for g in range(groups):
+        turned[pl.ds(g * LANES, LANES), :] = (
+            ret_y[pl.ds(2 * g, 2)].reshape(LANES, LANES).T
+        )
+    total = None
+    for z in range(8):
+        left = (
+            turned[pl.ds(2 * z, 8 * groups, stride=16), :]
+            + turned[pl.ds(2 * z + 1, 8 * groups, stride=16), :]
+        )
+        right = pick(
+            (k // 32 == (n % 256) // 64)
+            & ((k % 32) // 16 == n // 256)
+            & (n % 64 == ((k % 16) // 2) * 8 + z)
+        )
+        part = product(split(left), right)
+        total = part if total is None else total + part
+    for b in range(slots):
+        for way in range(2):
+            g, at = b // 2, (b % 2) * 2 + way
+            v = total[g * 8 : g * 8 + 8, at * 64 : at * 64 + 64]
+            w = total[g * 8 + way : g * 8 + way + 1, 256 + at * 64 : 256 + at * 64 + 64]
+            out[b, 2 + way, pl.ds(0, 8), :] = jnp.where(mask(b, 8), 0.0, v)
+            out[b, 2 + way, pl.ds(8, 1), :] = jnp.where(mask(b, 1), 0.0, w)
+
+    k, n = grid(LANES, 256)
+    total = [None] * groups
+    for g in range(groups):
+        turned[pl.ds(g * LANES, LANES), :] = (
+            ret_z[pl.ds(2 * g, 2)].reshape(LANES, LANES).T
+        )
+    for y in range(4):
+        right = pick(
+            (k // 32 == n // 64)
+            & (n % 64 == ((k % 16) // 2) * 8 + ((k % 32) // 16) * 4 + y)
+        )
+        for g in range(groups):
+            base = g * LANES + 32 * y
+            left = turned[pl.ds(base, 16), :] + turned[pl.ds(base + 16, 16), :]
+            part = product(split(left), right)
+            total[g] = part if total[g] is None else total[g] + part
+    for b in range(slots):
+        for way in range(2):
+            at = (b % 2) * 2 + way
+            v = total[b // 2][0:9, at * 64 : at * 64 + 64]
+            out[b, 4 + way] = jnp.where(mask(b, 9), 0.0, v)
+
+
+def rows_of(array):
+    slots, k, cells = array.shape
+    v = array.reshape(slots, k, cells // LANES, LANES).transpose(1, 2, 0, 3)
+    return v.reshape(-1, LANES)
+
+
+def array_of(rows, slots, k):
+    v = rows.reshape(k, -1, slots, LANES).transpose(2, 0, 1, 3)
+    return v.reshape(slots, k, -1)
 
 
 def local(
@@ -611,9 +718,9 @@
     outs = pl.pallas_call(
         kernel,
         out_shape=(
-            shape(populations.shape, F32),
-            shape(scalars.shape, F32),
-            shape((slots, 2, 18, LANES), F32),
+            shape((slots * 27 * ROWS, LANES), F32),
+            shape((slots * 9 * ROWS, LANES), F32),
+            shape((2, slots, 2, 16, LANES), F32),
             shape((slots, 2, 32, LANES), F32),
             shape((slots, 2, 32, LANES), F32),
         ),
@@ -627,7 +734,7 @@
             pltpu.VMEM((slots, SCA_ROWS, LANES), F32),
             pltpu.VMEM((slots, SCA_ROWS, LANES), F32),
             pltpu.VMEM((slots * 4 * ROWS, LANES), F32),
-            pltpu.VMEM((slots * 4 * ROWS, LANES), F32),
+            pltpu.VMEM((3, slots, 9 * ROWS, LANES), F32),
             pltpu.VMEM((layer + 1, XR, LANES), F32),
             pltpu.VMEM((layer + 1, XR, LANES), F32),
             pltpu.VMEM((layer, YR, LANES), F32),
@@ -657,24 +764,24 @@
         relax_rates,
         diffusivity,
         stoichiometry,
-        populations,
-        scalars,
-        coarse_old,
-        coarse_new,
+        rows_of(populations),
+        rows_of(scalars),
+        rows_of(coarse_old),
+        rows_of(coarse_new),
     )
     new_populations, new_scalars, ret_x, ret_y, ret_z = outs
-    x = ret_x.reshape(slots, 2, 2, 9, 4, 2, 8, 2).sum(axis=(5, 7))
-    x = x.transpose(0, 1, 3, 2, 4, 5).reshape(slots, 2, 9, 64)
-    y = ret_y.reshape(slots, 2, 2, 8, 2, 8, 8, 2).sum(axis=(4, 7))
-    y8 = jnp.stack([y[:, 0, 1, :, 0], y[:, 1, 1, :, 1]], axis=1)
-    y = jnp.concatenate([y[:, :, 0], y8[:, :, :, None]], axis=3)
-    y = y.transpose(0, 1, 3, 2, 4).reshape(slots, 2, 9, 64)
-    z = ret_z.reshape(slots, 2, 2, 8, 2, 4, 2, 16).sum(axis=(4, 6))[..., :9]
-    z = z.transpose(0, 1, 5, 3, 2, 4).reshape(slots, 2, 9, 64)
-    own = lax.dynamic_slice_in_dim(levels, lax.axis_index("blk") * slots, slots)
-    back = 0.25 * jnp.concatenate([x, y, z], axis=1).reshape(slots, -1)
-    back = jnp.where((own == 1)[:, None], 0.0, back)
-    return new_populations, new_scalars, back
+    back = pl.pallas_call(
+        means_kernel,
+        out_shape=shape((slots, 6, 9, 64), F32),
+        in_specs=[smem] + [vmem] * 3,
+        out_specs=vmem,
+        scratch_shapes=[pltpu.VMEM((slots // 2 * LANES, LANES), F32)],
+    )(levels, ret_x, ret_y, ret_z)
+    return (
+        array_of(new_populations, slots, 27),
+        array_of(new_scalars, slots, 9),
+        back.reshape(slots, -1),
+    )
 
 
 def solution(mesh):

time: 85.9 us -> 56.7 us (0.66)
  local copies, waits for them, and re-layouts: 21.4 us -> 5.4 us
  other arithmetic: 9.44 us -> 0 us
  Pallas kernels: 53.7 us -> 50.2 us
    unnamed x16 -> x4, local copies, waits for them, and re-layouts: 13.4 us -> 3.75 us
    reduce_sum x3 -> x0, other arithmetic: 7.63 us -> none  [the longest x1 5.6 us: local(): y = ret_y.reshape(slots, 2, 2, 8, 2, 8, 8, 2).sum(axis=(4, 7))]
    pallas_call x1 -> x2, Pallas kernels: 53.7 us -> 50.2 us  [the longest x1 47.5 us: local(): pl.pallas_call(kernel, out_shape=(shape((slots * 27 * ROWS, LANES), F32),...]
    pallas_call x2 -> x0, local copies, waits for them, and re-layouts: 2.83 us -> none  [local(): pl.pallas_call(kernel, out_shape=(shape(populations.shape, F32), shape(sc...]
    squeeze x2 -> x0, local copies, waits for them, and re-layouts: 1.03 us -> none  [local(): y = jnp.concatenate([y[:, :, 0], y8[:, :, :, None]], axis=3)]
    broadcast_in_dim x1 -> x0, local copies, waits for them, and re-layouts: 1.02 us -> none  [local(): y = jnp.concatenate([y[:, :, 0], y8[:, :, :, None]], axis=3)]
    eq x1 -> x0, other arithmetic: 0.86 us -> none  [local(): back = jnp.where((own == 1)[:, None], 0.0, back)]
    reshape x5 -> x1, local copies, waits for them, and re-layouts: 2.47 us -> 1.65 us  [local(): back.reshape(slots, -1)]
where the time goes in v2:
time: 56.7 us; the launch traced here: 56.2 us
  Pallas kernels  50.2 us (89%)
  local copies, waits for them, and re-layouts  5.4 us (10%)
  between operations  0.64 us (1%)
    pallas_call x1, Pallas kernels, local(): pl.pallas_call(kernel, out_shape=(shape((slots * 27 * ROWS, LANES), F32),...  47.5 us
    unnamed x4, local copies, waits for them, and re-layouts  3.75 us
    pallas_call x1, Pallas kernels, local(): pl.pallas_call(means_kernel, out_shape=shape((slots, 6, 9, 64), F32), in_...  2.68 us
    reshape x1, local copies, waits for them, and re-layouts, local(): back.reshape(slots, -1)  1.65 us

profile of v2, /device:TPU:0, one launch (start us, length us, event | category | flops | bytes accessed | tf_op | source)
XLA Modules:
  0.0 56.2 jit_solution(16463203939699048385)
XLA Ops:
  0.6 47.5 %shard_map.112 = (f32[3456,128]{1,0:T(8,128)}, f32[1152,128]{1,0:T(8,128)}, f32[2,4,2,16,128]{4,3,2,1,0:T(8,128)}, f32[4,2,32,128]{3,2,1,0:T(8,128)}, f32[4,2,32,128]{3,2,1,0:T(8,128)}) custom-call(s32[128]{0:T(128)} %levels.3, s32[4,6]{1,0:T(4,128)} %neighbours.1, f32[27]{0:T(128)} %rates.1, f32[9]{0:T(128)} %diffusivity.1, f32[9]{0:T(128)} %stoichiometry.1, ...), custom_call_target="tpu_custom_call" | custom-call | tf_op jit(solution)/shard_map/pallas_call | solution.py:718
  48.2 2.7 %shard_map.113 = f32[4,6,9,64]{3,2,1,0:T(8,128)} custom-call(s32[128]{0:T(128)} %levels.3, f32[2,4,2,16,128]{4,3,2,1,0:T(8,128)} %get-tuple-element.10.ret_x, f32[4,2,32,128]{3,2,1,0:T(8,128)} %get-tuple-element.11.ret_y, f32[4,2,32,128]{3,2,1,0:T(8,128)} %get-tuple-element.12.ret_z), custom_call_target="tpu_custom_call" | custom-call | tf_op jit(solution)/shard_map/pallas_call | solution.py:773
  50.8 1.6 %reshape.57 = f32[4,3456]{1,0:T(4,128)} reshape(f32[4,6,9,64]{3,2,1,0:T(8,128)} %shard_map.113) | data formatting | bytes 110592 | tf_op jit(solution)/shard_map/reshape | solution.py:783
  52.5 0.0 copy-start
  52.5 2.9 %copy.26 = f32[4,27,4096]{2,0,1:T(4,128)} copy(f32[4,27,4096]{2,0,1:T(4,128)} %bitcast.30) | data formatting | bytes 3538944
  55.4 0.0 copy-done
  55.4 0.8 %copy.27 = f32[4,9,4096]{2,0,1:T(4,128)} copy(f32[4,9,4096]{2,0,1:T(4,128)S(1)} %bitcast.32) | data formatting | bytes 1179648
Async XLA Ops:
  52.5 2.9 %copy-start = (f32[1152,128]{1,0:T(8,128)S(1)}, f32[1152,128]{1,0:T(8,128)}, u32[]{:S(2)}) copy-start(f32[1152,128]{1,0:T(8,128)} %get-tuple-element.9) | copy-start | bytes 1769476

commit v3 on v2

--- a/solution.py
+++ b/solution.py
@@ -166,10 +166,10 @@
     below = lax.rem(layer + layers - 1, layers)
     mine = core * slots
     around = 2 * slots
-    mesh_targets = ((2 * above, 2 * above + 1), (2 * below, 2 * below + 1))
+    mesh_targets = (2 * above + core, 2 * below + core)
 
     barrier = pltpu.get_barrier_semaphore()
-    for device in (partner,) + mesh_targets[0] + mesh_targets[1]:
+    for device in (partner,) + mesh_targets:
         pl.semaphore_signal(barrier, inc=1, device_id=(device,), device_id_type=MESH)
 
     counter = [0, 0]
@@ -205,38 +205,36 @@
         return wait
 
     def send_layers(source, target):
-        waits = []
+        copies = []
         for way in range(2):
-            r = counter[1]
-            counter[1] += 2
-            for core_to in range(2):
-                s = counter[0]
-                counter[0] += 1
-                copy = pltpu.make_async_remote_copy(
-                    src_ref=source.at[way],
-                    dst_ref=target.at[way, pl.ds(mine, slots)],
-                    send_sem=send_sem.at[s],
-                    recv_sem=recv_sem.at[r + core],
-                    device_id=(mesh_targets[way][core_to],),
-                    device_id_type=MESH,
-                )
-                copy.start()
-                waits.append(copy.wait_send)
-                arrival = pltpu.make_async_remote_copy(
-                    src_ref=source.at[way],
-                    dst_ref=target.at[way, pl.ds(core_to * slots, slots)],
-                    send_sem=send_sem.at[s],
-                    recv_sem=recv_sem.at[r + core_to],
-                    device_id=(mesh_targets[way][core_to],),
-                    device_id_type=MESH,
-                )
-                waits.append(arrival.wait_recv)
-
-        def wait():
-            for w in waits:
-                w()
-
-        return wait
+            s, r = counter[0], counter[1]
+            counter[0] += 1
+            counter[1] += 1
+            copy = pltpu.make_async_remote_copy(
+                src_ref=source.at[way],
+                dst_ref=target.at[way, pl.ds(mine, slots)],
+                send_sem=send_sem.at[s],
+                recv_sem=recv_sem.at[r],
+                device_id=(mesh_targets[way],),
+                device_id_type=MESH,
+            )
+            copy.start()
+            copies.append(copy)
+
+        def relay():
+            waits = []
+            for way in range(2):
+                copies[way].wait_recv()
+                waits.append(send_partner(target.at[way]))
+
+            def wait():
+                for way in range(2):
+                    copies[way].wait_send()
+                    waits[way]()
+
+            return wait
+
+        return relay
 
     def each_block(body):
         def wrapped(b, carry):
@@ -263,28 +261,41 @@
 
     each_block(unpack_in)
 
-    def spread_coarse(target, average):
+    def spread_values(average):
         a = 0.5 * (old[...] + new[...]) if average else old[...]
         row = lax.broadcasted_iota(jnp.int32, (LANES, LANES), 0)
         col = lax.broadcasted_iota(jnp.int32, (LANES, LANES), 1)
         want = (col // 32) * 8 + (col % 16) // 2
         parts = split(a)
         for variant in range(4):
-            parity, half = variant // 2, variant % 2
-            pick = jnp.where(row == want + parity * 64 + half * 32, 1.0, 0.0).astype(jnp.bfloat16)
-            res[pl.ds(0, a.shape[0]), :] = product(parts, pick)
-
-            def scatter(b, carry):
+            at = variant // 2 * 64 + variant % 2 * 32
+            pick = jnp.where(row == want + at, 1.0, 0.0).astype(jnp.bfloat16)
+            res[variant, pl.ds(0, a.shape[0]), :] = product(parts, pick)
+
+    def spread_rows(target, b, variant, chunk, xs):
+        v = res[variant, pl.ds(chunk * slots + b, 27, stride=4 * slots), :]
+        for x in xs:
+            target[b, pl.ds(variant % 2 * HALF + x, 27, stride=ROWS), :] = v
+
+    def spread_ends(target):
+        def body(b):
+            for half in range(2):
+                spread_rows(target, b, half, 0, (0,))
+                spread_rows(target, b, 2 + half, 3, (15,))
+
+        each_block(body)
+
+    def spread_all(target):
+        def body(b):
+            for variant in range(4):
                 for chunk in range(4):
-                    v = res[pl.ds(chunk * slots + b, 27, stride=4 * slots), :]
-                    x = 2 * (2 * chunk + parity)
-                    target[b, pl.ds(half * HALF + x, 27, stride=ROWS), :] = v
-                    target[b, pl.ds(half * HALF + x + 1, 27, stride=ROWS), :] = v
-                return carry
-
-            lax.fori_loop(0, slots, scatter, 0)
-
-    spread_coarse(up0, False)
+                    x = 2 * (2 * chunk + variant // 2)
+                    spread_rows(target, b, variant, chunk, (x, x + 1))
+
+        each_block(body)
+
+    spread_values(False)
+    spread_ends(up0)
 
     def population_load(b, spread):
         fine = fine_of(b)
@@ -530,7 +541,7 @@
 
         each_block(body)
 
-    pl.semaphore_wait(barrier, 5)
+    pl.semaphore_wait(barrier, 3)
     last_wait = None
     for substep in range(2):
         spread = (up0, up1)[substep]
@@ -557,11 +568,12 @@
 
             each_block(pack_return)
             wait_r = send_partner(rxy)
-            wait_rz = send_layers(rz_out, rz)
+            relay_rz = send_layers(rz_out, rz)
         else:
             each_block(pack_scalars)
             wait_s = send_partner(cs)
-            wait_sz = send_layers(cs_out, cs_z)
+            relay_sz = send_layers(cs_out, cs_z)
+            spread_all(up0)
         each_block(shift_x)
         wait()
         each_block(lambda b: enter_x(b, cx))
@@ -570,18 +582,23 @@
         if substep == 1:
             each_block(pack_scalars)
             wait_s = send_partner(cs)
-            wait_sz = send_layers(cs_out, cs_z)
+            relay_sz = send_layers(cs_out, cs_z)
         else:
-            spread_coarse(up1, True)
+            spread_values(True)
+            spread_all(up1)
         each_block(shift_y)
         wait()
         each_block(lambda b: enter_y(b, cy))
         each_block(lambda b: pack_z(population_load(b, spread), putter_z(cz_out, b)))
-        wait = send_layers(cz_out, cz)
+        relay = send_layers(cz_out, cz)
+        wait_sz = relay_sz()
         each_block(shift_z)
         wait_s()
         wait_sz()
+        if substep == 1:
+            wait_rz = relay_rz()
         prepare(source, target, cs, cs_z)
+        wait = relay()
         wait()
         each_block(lambda b: enter_z(b, cz))
         finish(target)
@@ -733,7 +750,7 @@
             pltpu.VMEM((slots, POP_ROWS, LANES), F32),
             pltpu.VMEM((slots, SCA_ROWS, LANES), F32),
             pltpu.VMEM((slots, SCA_ROWS, LANES), F32),
-            pltpu.VMEM((slots * 4 * ROWS, LANES), F32),
+            pltpu.VMEM((4, slots * 4 * ROWS, LANES), F32),
             pltpu.VMEM((3, slots, 9 * ROWS, LANES), F32),
             pltpu.VMEM((layer + 1, XR, LANES), F32),
             pltpu.VMEM((layer + 1, XR, LANES), F32),

time: 56.7 us -> 48.4 us (0.85)
  Pallas kernels: 50.2 us -> 42.1 us
    pallas_call x1, Pallas kernels: 47.5 us -> 39.4 us  [local(): pl.pallas_call(kernel, out_shape=(shape((slots * 27 * ROWS, LANES), F32),...]
where the time goes in v3:
time: 48.4 us; the launch traced here: 48.1 us
  Pallas kernels  42.1 us (87%)
  local copies, waits for them, and re-layouts  5.4 us (11%)
  between operations  0.64 us (1%)
    pallas_call x1, Pallas kernels, local(): pl.pallas_call(kernel, out_shape=(shape((slots * 27 * ROWS, LANES), F32),...  39.4 us
    unnamed x4, local copies, waits for them, and re-layouts  3.75 us
    pallas_call x1, Pallas kernels, local(): pl.pallas_call(means_kernel, out_shape=shape((slots, 6, 9, 64), F32), in_...  2.68 us
    reshape x1, local copies, waits for them, and re-layouts, local(): back.reshape(slots, -1)  1.65 us

profile of v3, /device:TPU:0, one launch (start us, length us, event | category | flops | bytes accessed | tf_op | source)
XLA Modules:
  0.0 48.1 jit_solution(9076503128074918815)
XLA Ops:
  0.6 39.4 %shard_map.112 = (f32[3456,128]{1,0:T(8,128)}, f32[1152,128]{1,0:T(8,128)}, f32[2,4,2,16,128]{4,3,2,1,0:T(8,128)}, f32[4,2,32,128]{3,2,1,0:T(8,128)}, f32[4,2,32,128]{3,2,1,0:T(8,128)}) custom-call(s32[128]{0:T(128)} %levels.3, s32[4,6]{1,0:T(4,128)} %neighbours.1, f32[27]{0:T(128)} %rates.1, f32[9]{0:T(128)} %diffusivity.1, f32[9]{0:T(128)} %stoichiometry.1, ...), custom_call_target="tpu_custom_call" | custom-call | tf_op jit(solution)/shard_map/pallas_call | solution.py:735
  40.0 2.7 %shard_map.113 = f32[4,6,9,64]{3,2,1,0:T(8,128)} custom-call(s32[128]{0:T(128)} %levels.3, f32[2,4,2,16,128]{4,3,2,1,0:T(8,128)} %get-tuple-element.10.ret_x, f32[4,2,32,128]{3,2,1,0:T(8,128)} %get-tuple-element.11.ret_y, f32[4,2,32,128]{3,2,1,0:T(8,128)} %get-tuple-element.12.ret_z), custom_call_target="tpu_custom_call" | custom-call | tf_op jit(solution)/shard_map/pallas_call | solution.py:790
  42.7 1.6 %reshape.57 = f32[4,3456]{1,0:T(4,128)} reshape(f32[4,6,9,64]{3,2,1,0:T(8,128)} %shard_map.113) | data formatting | bytes 110592 | tf_op jit(solution)/shard_map/reshape | solution.py:800
  44.4 0.0 copy-start
  44.4 2.9 %copy.26 = f32[4,27,4096]{2,0,1:T(4,128)} copy(f32[4,27,4096]{2,0,1:T(4,128)} %bitcast.30) | data formatting | bytes 3538944
  47.3 0.0 copy-done
  47.3 0.8 %copy.27 = f32[4,9,4096]{2,0,1:T(4,128)} copy(f32[4,9,4096]{2,0,1:T(4,128)S(1)} %bitcast.32) | data formatting | bytes 1179648
Async XLA Ops:
  44.4 2.9 %copy-start = (f32[1152,128]{1,0:T(8,128)S(1)}, f32[1152,128]{1,0:T(8,128)}, u32[]{:S(2)}) copy-start(f32[1152,128]{1,0:T(8,128)} %get-tuple-element.9) | copy-start | bytes 1769476

commit v4 on v3

--- a/solution.py
+++ b/solution.py
@@ -558,6 +558,9 @@
         collide(substep == 0)
         each_block(lambda b: pack_x(population_load(b, spread), putter(cx, mine + b)))
         wait = send_partner(cx)
+        each_block(pack_scalars)
+        wait_s = send_partner(cs)
+        relay_sz = send_layers(cs_out, cs_z)
         if substep == 1:
 
             def pack_return(b):
@@ -567,12 +570,7 @@
                 pack_z(load, putter_z(rz_out, b))
 
             each_block(pack_return)
-            wait_r = send_partner(rxy)
-            relay_rz = send_layers(rz_out, rz)
         else:
-            each_block(pack_scalars)
-            wait_s = send_partner(cs)
-            relay_sz = send_layers(cs_out, cs_z)
             spread_all(up0)
         each_block(shift_x)
         wait()
@@ -580,9 +578,7 @@
         each_block(lambda b: pack_y(population_load(b, spread), putter(cy, mine + b)))
         wait = send_partner(cy)
         if substep == 1:
-            each_block(pack_scalars)
-            wait_s = send_partner(cs)
-            relay_sz = send_layers(cs_out, cs_z)
+            wait_r = send_partner(rxy)
         else:
             spread_values(True)
             spread_all(up1)
@@ -591,15 +587,17 @@
         each_block(lambda b: enter_y(b, cy))
         each_block(lambda b: pack_z(population_load(b, spread), putter_z(cz_out, b)))
         relay = send_layers(cz_out, cz)
+        if substep == 1:
+            relay_rz = send_layers(rz_out, rz)
         wait_sz = relay_sz()
         each_block(shift_z)
         wait_s()
         wait_sz()
-        if substep == 1:
-            wait_rz = relay_rz()
         prepare(source, target, cs, cs_z)
         wait = relay()
         wait()
+        if substep == 1:
+            wait_rz = relay_rz()
         each_block(lambda b: enter_z(b, cz))
         finish(target)
     wait_r()
@@ -638,6 +636,11 @@
     def mask(b, rows):
         return jnp.broadcast_to(levels[first + b], (rows, 64)) == 1
 
+    def put(b, side, start, values):
+        for p in range(values.shape[0]):
+            at = (side * 9 + start + p) * 64
+            out[pl.ds(b, 1), pl.ds(at, 64)] = values[p : p + 1]
+
     def grid(rows, columns):
         return tuple(lax.broadcasted_iota(jnp.int32, (rows, columns), d) for d in range(2))
 
@@ -654,7 +657,7 @@
     for b in range(slots):
         for way in range(2):
             v = total[(b * 2 + way) * 16 : (b * 2 + way) * 16 + 9]
-            out[b, way] = jnp.where(mask(b, 9), 0.0, v)
+            put(b, way, 0, jnp.where(mask(b, 9), 0.0, v))
 
     k, n = grid(LANES, 512)
     for g in range(groups):
@@ -679,8 +682,8 @@
             g, at = b // 2, (b % 2) * 2 + way
             v = total[g * 8 : g * 8 + 8, at * 64 : at * 64 + 64]
             w = total[g * 8 + way : g * 8 + way + 1, 256 + at * 64 : 256 + at * 64 + 64]
-            out[b, 2 + way, pl.ds(0, 8), :] = jnp.where(mask(b, 8), 0.0, v)
-            out[b, 2 + way, pl.ds(8, 1), :] = jnp.where(mask(b, 1), 0.0, w)
+            put(b, 2 + way, 0, jnp.where(mask(b, 8), 0.0, v))
+            put(b, 2 + way, 8, jnp.where(mask(b, 1), 0.0, w))
 
     k, n = grid(LANES, 256)
     total = [None] * groups
@@ -702,7 +705,7 @@
         for way in range(2):
             at = (b % 2) * 2 + way
             v = total[b // 2][0:9, at * 64 : at * 64 + 64]
-            out[b, 4 + way] = jnp.where(mask(b, 9), 0.0, v)
+            put(b, 4 + way, 0, jnp.where(mask(b, 9), 0.0, v))
 
 
 def rows_of(array):
@@ -789,7 +792,7 @@
     new_populations, new_scalars, ret_x, ret_y, ret_z = outs
     back = pl.pallas_call(
         means_kernel,
-        out_shape=shape((slots, 6, 9, 64), F32),
+        out_shape=shape((slots, 6 * 9 * 64), F32),
         in_specs=[smem] + [vmem] * 3,
         out_specs=vmem,
         scratch_shapes=[pltpu.VMEM((slots // 2 * LANES, LANES), F32)],
@@ -797,7 +800,7 @@
     return (
         array_of(new_populations, slots, 27),
         array_of(new_scalars, slots, 9),
-        back.reshape(slots, -1),
+        back,
     )
 
 

time: 48.4 us -> 46.8 us (0.967)
  local copies, waits for them, and re-layouts: 5.4 us -> 3.75 us
    reshape x1 -> x0, local copies, waits for them, and re-layouts: 1.65 us -> none  [local(): back.reshape(slots, -1)]
where the time goes in v4:
time: 46.8 us; the launch traced here: 46.6 us
  Pallas kernels  42.2 us (90%)
  local copies, waits for them, and re-layouts  3.75 us (8%)
  between operations  0.64 us (1%)
    pallas_call x1, Pallas kernels, local(): pl.pallas_call(kernel, out_shape=(shape((slots * 27 * ROWS, LANES), F32),...  39.5 us
    unnamed x4, local copies, waits for them, and re-layouts  3.75 us
    pallas_call x1, Pallas kernels, local(): pl.pallas_call(means_kernel, out_shape=shape((slots, 6 * 9 * 64), F32), i...  2.65 us

profile of v4, /device:TPU:0, one launch (start us, length us, event | category | flops | bytes accessed | tf_op | source)
XLA Modules:
  0.0 46.6 jit_solution(676960664299526231)
XLA Ops:
  0.6 39.5 %shard_map.112 = (f32[3456,128]{1,0:T(8,128)}, f32[1152,128]{1,0:T(8,128)}, f32[2,4,2,16,128]{4,3,2,1,0:T(8,128)}, f32[4,2,32,128]{3,2,1,0:T(8,128)}, f32[4,2,32,128]{3,2,1,0:T(8,128)}) custom-call(s32[128]{0:T(128)} %levels.3, s32[4,6]{1,0:T(4,128)} %neighbours.1, f32[27]{0:T(128)} %rates.1, f32[9]{0:T(128)} %diffusivity.1, f32[9]{0:T(128)} %stoichiometry.1, ...), custom_call_target="tpu_custom_call" | custom-call | tf_op jit(solution)/shard_map/pallas_call | solution.py:738
  40.2 2.6 %shard_map.113 = f32[4,3456]{1,0:T(4,128)} custom-call(s32[128]{0:T(128)} %levels.3, f32[2,4,2,16,128]{4,3,2,1,0:T(8,128)} %get-tuple-element.10.ret_x, f32[4,2,32,128]{3,2,1,0:T(8,128)} %get-tuple-element.11.ret_y, f32[4,2,32,128]{3,2,1,0:T(8,128)} %get-tuple-element.12.ret_z), custom_call_target="tpu_custom_call" | custom-call | tf_op jit(solution)/shard_map/pallas_call | solution.py:793
  42.8 0.0 copy-start
  42.8 2.9 %copy.20 = f32[4,27,4096]{2,0,1:T(4,128)} copy(f32[4,27,4096]{2,0,1:T(4,128)} %bitcast.30) | data formatting | bytes 3538944
  45.8 0.0 copy-done
  45.8 0.8 %copy.21 = f32[4,9,4096]{2,0,1:T(4,128)} copy(f32[4,9,4096]{2,0,1:T(4,128)S(1)} %bitcast.32) | data formatting | bytes 1179648
Async XLA Ops:
  42.8 2.9 %copy-start = (f32[1152,128]{1,0:T(8,128)S(1)}, f32[1152,128]{1,0:T(8,128)}, u32[]{:S(2)}) copy-start(f32[1152,128]{1,0:T(8,128)} %get-tuple-element.9) | copy-start | bytes 1769476
